TPU v7x, 128 devices: a whole 4x4x4 slice. The times are simulated.
128 devices in a mesh: dp: 2 (over x_lo), expert: 64 (over y, z, x_hi, core).
Axes of the slice: x: 4 (x_hi: 2, x_lo: 2; x = x_hi * 2 + x_lo), y: 4, z: 4, core: 2. Of those that a mesh axis runs over, the one named last changes fastest.
Arguments:
- tokens: bfloat16 [16384, 2048], P(('dp', 'expert')), may hold values from -6 to 6
- cotangent: bfloat16 [16384, 2048], P(('dp', 'expert')), may hold values from -6 to 6
- expert_ids: int32 [16384, 4], P(('dp', 'expert')), may hold values from 0 to 63, all different within a row; in each aligned block of 128 rows (0 to 127, 128 to 255, ...) at most 12 rows name the same one
- combine: float32 [16384, 4], P(('dp', 'expert')), may hold values from 0.1 to 1
- placement: int32 [64], replicated, may hold values from 0 to 63, each once
- moves: int32 [64], replicated, may hold values from 0 to 1, as said below
- w_gate: bfloat16 [64, 2048, 768], P('expert'), may hold values from -0.125 to 0.125
- w_up: bfloat16 [64, 2048, 768], P('expert'), may hold values from -0.125 to 0.125
- w_down: bfloat16 [64, 768, 2048], P('expert'), may hold values from -0.21875 to 0.21875
Outputs:
- mixed: bfloat16 [16384, 2048], P(('dp', 'expert'))
- input_grad: bfloat16 [16384, 2048], P(('dp', 'expert'))
- grad_gate: float32 [64, 2048, 768], P('expert', 'dp')
- grad_up: float32 [64, 2048, 768], P('expert', 'dp')
- grad_down: float32 [64, 768, 2048], P('expert', 'dp')
Inputs may be any that keep to these rules, and one draw needn't show every extreme that they name: `expert_ids`: each row names 4 different experts. In the rows of one device no expert is named more than 12 times, a bound that some block reaches. `placement`: A permutation of the experts. moves[d] = moves[(d + 32) mod 64]; at least one pair exchanges and at least one does not.
All inputs are finite; a program needn't handle non-finite values.
Results may differ from a plain program's by a relative error of at most 0.0064.
Values may be sent and summed in bfloat16 or wider, within the bound.
A program may use at most 192 MiB of HBM per device.

v0:
```python
import jax
import jax.numpy as jnp
from jax import lax
from jax.sharding import PartitionSpec as P


def swapped(array, axis, apart):
    return lax.ppermute(array, axis, [(i, i ^ 1 << apart) for i in range(lax.axis_size(axis))])


def body(tokens, cotangent, expert_ids, combine, placement, moves, w_gate, w_up, w_down):
    owner_count = lax.axis_size("expert")
    my_index = lax.axis_index("expert")
    tok_rows, width = tokens.shape
    choose_count = expert_ids.shape[1]
    flat_count = tok_rows * choose_count
    capacity = 3 * flat_count // (2 * owner_count)
    pair_bit = owner_count.bit_length() - 2
    slot_ids = jnp.arange(owner_count, dtype=jnp.int32)
    held_expert = jnp.where(moves == 1, jnp.roll(placement, owner_count // 2), placement)
    my_move = jnp.sum(jnp.where(slot_ids == my_index, moves, 0))
    exchanged = my_move == 1
    moved = swapped((w_gate, w_up, w_down), "expert", pair_bit)
    gate_weight = jnp.where(exchanged, moved[0][0], w_gate[0])
    up_weight = jnp.where(exchanged, moved[1][0], w_up[0])
    down_weight = jnp.where(exchanged, moved[2][0], w_down[0])
    flat_ids = expert_ids.reshape(-1)
    flat_weights = combine.reshape(-1)
    token_of = jnp.arange(flat_count, dtype=jnp.int32) // choose_count
    destination = jnp.sum(
        jnp.where(held_expert[None, :] == flat_ids[:, None], slot_ids[None, :], 0), axis=1
    )
    one_hot = (destination[:, None] == slot_ids[None, :]).astype(jnp.int32)
    earlier = jnp.cumsum(one_hot, axis=0) - one_hot
    slot_rank = jnp.sum(earlier * one_hot, axis=1)
    position = destination * capacity + slot_rank
    buffer_rows = owner_count * capacity
    source_row = jnp.zeros((buffer_rows,), jnp.int32).at[position].set(token_of)
    slot_weight = jnp.zeros((buffer_rows,), jnp.float32).at[position].set(flat_weights)
    live_rows = jnp.zeros((buffer_rows,), jnp.float32).at[position].set(1.0)
    send_inputs = jnp.where(
        live_rows[:, None] > 0.0, tokens[source_row], jnp.zeros((), jnp.bfloat16)
    )
    send_grads = (slot_weight[:, None] * cotangent[source_row].astype(jnp.float32)).astype(
        jnp.bfloat16
    )
    arrived = (
        lax.all_to_all(
            send_inputs.reshape(owner_count, capacity, width),
            "expert",
            split_axis=0,
            concat_axis=0,
            tiled=True,
        ),
        lax.all_to_all(
            send_grads.reshape(owner_count, capacity, width),
            "expert",
            split_axis=0,
            concat_axis=0,
            tiled=True,
        ),
    )
    row_inputs = arrived[0].reshape(buffer_rows, width)
    out_grad = arrived[1].reshape(buffer_rows, width)
    contract_rows = (((0,), (0,)), ((), ()))
    contract_last = (((1,), (1,)), ((), ()))
    gate_pre = jnp.dot(row_inputs, gate_weight, preferred_element_type=jnp.float32)
    up_pre = jnp.dot(row_inputs, up_weight, preferred_element_type=jnp.float32)
    sigma = jax.nn.sigmoid(gate_pre)
    hidden = (gate_pre * sigma * up_pre).astype(jnp.bfloat16)
    expert_out = jnp.dot(hidden, down_weight, preferred_element_type=jnp.float32).astype(
        jnp.bfloat16
    )
    hidden_grad = lax.dot_general(
        out_grad, down_weight, contract_last, preferred_element_type=jnp.float32
    )
    gate_grad = (hidden_grad * up_pre * sigma * (1.0 + gate_pre * (1.0 - sigma))).astype(
        jnp.bfloat16
    )
    up_grad = (hidden_grad * gate_pre * sigma).astype(jnp.bfloat16)
    row_grad = (
        lax.dot_general(gate_grad, gate_weight, contract_last, preferred_element_type=jnp.float32)
        + lax.dot_general(up_grad, up_weight, contract_last, preferred_element_type=jnp.float32)
    ).astype(jnp.bfloat16)
    returned = (
        lax.all_to_all(
            expert_out.reshape(owner_count, capacity, width),
            "expert",
            split_axis=0,
            concat_axis=0,
            tiled=True,
        ),
        lax.all_to_all(
            row_grad.reshape(owner_count, capacity, width),
            "expert",
            split_axis=0,
            concat_axis=0,
            tiled=True,
        ),
    )
    out_rows = returned[0].reshape(buffer_rows, width)[position]
    grad_rows = returned[1].reshape(buffer_rows, width)[position]
    mixed = jnp.sum(
        combine[:, :, None] * out_rows.reshape(tok_rows, choose_count, width).astype(jnp.float32),
        axis=1,
    )
    input_grad = jnp.sum(
        grad_rows.reshape(tok_rows, choose_count, width).astype(jnp.float32), axis=1
    )
    g_gate = lax.dot_general(
        row_inputs, gate_grad, contract_rows, preferred_element_type=jnp.float32
    )
    g_up = lax.dot_general(row_inputs, up_grad, contract_rows, preferred_element_type=jnp.float32)
    g_down = lax.dot_general(hidden, out_grad, contract_rows, preferred_element_type=jnp.float32)
    summed = (
        lax.psum_scatter(g_gate, "dp", scatter_dimension=0, tiled=True),
        lax.psum_scatter(g_up, "dp", scatter_dimension=0, tiled=True),
        lax.psum_scatter(g_down, "dp", scatter_dimension=0, tiled=True),
    )
    scale = 1.0 / lax.axis_size("dp")
    share_gate = summed[0] * scale
    share_up = summed[1] * scale
    share_down = summed[2] * scale
    return (
        mixed.astype(jnp.bfloat16),
        input_grad.astype(jnp.bfloat16),
        share_gate[None],
        share_up[None],
        share_down[None],
    )


def solution(mesh):
    return jax.shard_map(
        body,
        mesh=mesh,
        in_specs=(
            P(("dp", "expert"), None),
            P(("dp", "expert"), None),
            P(("dp", "expert"), None),
            P(("dp", "expert"), None),
            P(),
            P(),
            P("expert", None, None),
            P("expert", None, None),
            P("expert", None, None),
        ),
        out_specs=(
            P(("dp", "expert"), None),
            P(("dp", "expert"), None),
            P("expert", "dp", None),
            P("expert", "dp", None),
            P("expert", "dp", None),
        ),
        check_vma=False,
    )
```

profile of v0, /device:TPU:1, one launch (start us, length us, event | category | flops | bytes accessed | tf_op | source)
XLA Modules:
  0.0 731.1 jit_solution(7274820796856286306)
XLA Ops:
  9.0 1.4 fusion.23
  10.4 1.2 reduce-window.6
  12.1 2.4 scatter_custom_fusion.1
  14.6 4.2 gather_fusion.2
  18.8 6.5 reshape.120
  25.5 2.4 scatter_custom_fusion.2
  28.0 5.9 multiply_convert_fusion
  33.9 12.8 %all-to-all-start.2 = ((bf16[64,12,2048]{2,1,0:T(8,128)(2,1)}), bf16[64,12,2048]{2,1,0:T(8,128)(2,1)}, u32[]{:S(2)}, u32[]{:S(2)}) async-start(bf16[64,12,2048]{2,1,0:T(8,128)(2,1)} %multiply_convert_fusion), calls=%async_computation.2 | async-start | bytes 8388608 | tf_op jit(solution)/shard_map/all_to_all | solution.py:55
  46.7 3.1 collective-permute-start.2
  49.8 4.2 gather_fusion
  54.0 6.1 gather.15
  60.1 2.4 scatter_custom_fusion
  62.6 4.5 broadcast_select_fusion
  67.2 33.2 %all-to-all-done.2 = bf16[64,12,2048]{2,1,0:T(8,128)(2,1)} async-done(((bf16[64,12,2048]{2,1,0:T(8,128)(2,1)}), bf16[64,12,2048]{2,1,0:T(8,128)(2,1)}, u32[]{:S(2)}, u32[]{:S(2)}) %all-to-all-start.2) | async-done | bytes 3145760 | tf_op jit(solution)/shard_map/all_to_all | solution.py:55
  100.3 74.0 %all-to-all-start = ((bf16[64,12,2048]{2,1,0:T(8,128)(2,1)}), bf16[64,12,2048]{2,1,0:T(8,128)(2,1)}, u32[]{:S(2)}, u32[]{:S(2)}) async-start(bf16[64,12,2048]{2,1,0:T(8,128)(2,1)} %broadcast_select_fusion), calls=%async_computation | async-start | bytes 8388608 | tf_op jit(solution)/shard_map/all_to_all | solution.py:48
  174.4 3.1 collective-permute-start.1
  178.4 4.7 reshape.115
  183.2 44.9 %all-to-all-done = bf16[64,12,2048]{2,1,0:T(8,128)(2,1)} async-done(((bf16[64,12,2048]{2,1,0:T(8,128)(2,1)}), bf16[64,12,2048]{2,1,0:T(8,128)(2,1)}, u32[]{:S(2)}, u32[]{:S(2)}) %all-to-all-start) | async-done | bytes 3145760 | tf_op jit(solution)/shard_map/all_to_all | solution.py:48
  228.1 6.2 reshape.111
  234.2 4.7 fusion
  238.9 52.2 %collective-permute-done.1 = bf16[1,2048,768]{2,1,0:T(8,128)(2,1)} collective-permute-done((bf16[1,2048,768]{2,1,0:T(8,128)(2,1)}, bf16[1,2048,768]{2,1,0:T(8,128)(2,1)}, u32[]{:S(2)}, u32[]{:S(2)}) %collective-permute-start.1) | collective-permute-done | bytes 3145760 | tf_op jit(solution)/shard_map/ppermute | solution.py:8
  291.1 4.5 fusion.5
  295.6 62.9 %collective-permute-done = bf16[1,2048,768]{2,1,0:T(8,128)(2,1)} collective-permute-done((bf16[1,2048,768]{2,1,0:T(8,128)(2,1)}, bf16[1,2048,768]{2,1,0:T(8,128)(2,1)}, u32[]{:S(2)}, u32[]{:S(2)}) %collective-permute-start) | collective-permute-done | bytes 3145760 | tf_op jit(solution)/shard_map/ppermute | solution.py:8
  358.5 6.7 multiply_convert_fusion.2
  366.3 4.6 fusion.25
  371.0 7.5 %fusion.26 = f32[2048,768]{1,0:T(8,128)} fusion(bf16[768,2048]{1,0:T(8,128)(2,1)} %reshape.111, bf16[768,768]{1,0:T(8,128)(2,1)} %get-tuple-element.7), kind=kOutput, calls=%fused_computation.66 | convolution fusion | flops 2415919104 | bytes 10616832 | tf_op jit(solution)/shard_map/dot_general | solution.py:113
  378.8 5.8 fusion.27
  384.7 4.9 convolution_convert_fusion
  389.5 2.8 reshape.112
  392.3 26.6 %all-to-all-start.1 = ((bf16[64,12,2048]{2,1,0:T(8,128)(2,1)}), bf16[64,12,2048]{2,1,0:T(8,128)(2,1)}, u32[]{:S(2)}, u32[]{:S(2)}) async-start(bf16[64,12,2048]{2,1,0:T(8,128)(2,1)} %reshape.112), calls=%async_computation.1 | async-start | bytes 8388608 | tf_op jit(solution)/shard_map/all_to_all | solution.py:86
  418.9 4.4 fusion.3
  423.3 4.8 add_convert_fusion
  428.1 2.7 reshape.116
  430.8 86.4 %all-to-all-done.1 = bf16[64,12,2048]{2,1,0:T(8,128)(2,1)} async-done(((bf16[64,12,2048]{2,1,0:T(8,128)(2,1)}), bf16[64,12,2048]{2,1,0:T(8,128)(2,1)}, u32[]{:S(2)}, u32[]{:S(2)}) %all-to-all-start.1) | async-done | bytes 3145760 | tf_op jit(solution)/shard_map/all_to_all | solution.py:86
  517.2 5.5 all-to-all-start.3
  522.7 5.0 reshape.113
  527.8 3.3 gather_fusion.1
  531.0 4.8 reshape.119
  535.8 81.7 %all-to-all-done.3 = bf16[64,12,2048]{2,1,0:T(8,128)(2,1)} async-done(((bf16[64,12,2048]{2,1,0:T(8,128)(2,1)}), bf16[64,12,2048]{2,1,0:T(8,128)(2,1)}, u32[]{:S(2)}, u32[]{:S(2)}) %all-to-all-start.3) | async-done | bytes 3145760 | tf_op jit(solution)/shard_map/all_to_all | solution.py:93
  617.5 4.8 reshape.117
  622.3 3.3 gather_fusion.3
  625.6 2.8 reshape.118
  628.3 3.9 reduce_sum.52
  632.2 6.2 multiply_reduce_fusion
  638.4 3.8 multiply_bitcast_fusion.2
  642.2 3.8 multiply_bitcast_fusion.1
  646.0 74.2 %reduce-scatter.8.cloned.1.call-done = f32[384,2048]{1,0:T(8,128)} async-done(((f32[768,2048]{1,0:T(8,128)}), f32[384,2048]{1,0:T(8,128)}) %reduce-scatter.8.cloned.1.call-update) | async-done | bytes 3145744 | tf_op jit(solution)/shard_map/reduce_scatter | solution.py:118
  720.2 3.9 multiply_bitcast_fusion
  (47 shorter events, 4.4 us)
Async XLA Ops:
  7.2 7.4 %copy-start = (bf16[128,2048]{1,0:T(8,128)(2,1)S(1)}, bf16[128,2048]{1,0:T(8,128)(2,1)}, u32[]{:S(2)}) copy-start(bf16[128,2048]{1,0:T(8,128)(2,1)} %param.10) | copy-start | bytes 1572868
  18.8 6.5 copy-start.4
  33.9 15.9 %copy-start.2 = (bf16[128,2048]{1,0:T(8,128)(2,1)S(1)}, bf16[128,2048]{1,0:T(8,128)(2,1)}, u32[]{:S(2)}) copy-start(bf16[128,2048]{1,0:T(8,128)(2,1)} %param.9) | copy-start | bytes 1572868
  33.9 66.4 %all-to-all-start.2 = ((bf16[64,12,2048]{2,1,0:T(8,128)(2,1)}), bf16[64,12,2048]{2,1,0:T(8,128)(2,1)}, u32[]{:S(2)}, u32[]{:S(2)}) async-start(bf16[64,12,2048]{2,1,0:T(8,128)(2,1)} %multiply_convert_fusion), calls=%async_computation.2 | async-start | bytes 8388608 | tf_op jit(solution)/shard_map/all_to_all | solution.py:55
  46.7 187.5 %collective-permute-start.2 = (bf16[1,768,2048]{2,1,0:T(8,128)(2,1)}, bf16[1,768,2048]{2,1,0:T(8,128)(2,1)}, u32[]{:S(2)}, u32[]{:S(2)}) collective-permute-start(bf16[1,768,2048]{2,1,0:T(8,128)(2,1)} %param.17), channel_id=1, source_target_pairs={{0,32},{1,33},{2,34},{3,35},{4,36},{5,37},{6,38},{7,39},{8,40},{9,... | collective-permute-start | bytes 9437192 | tf_op jit(solution)/shard_map/ppermute | solution.py:8
  100.3 127.7 %all-to-all-start = ((bf16[64,12,2048]{2,1,0:T(8,128)(2,1)}), bf16[64,12,2048]{2,1,0:T(8,128)(2,1)}, u32[]{:S(2)}, u32[]{:S(2)}) async-start(bf16[64,12,2048]{2,1,0:T(8,128)(2,1)} %broadcast_select_fusion), calls=%async_computation | async-start | bytes 8388608 | tf_op jit(solution)/shard_map/all_to_all | solution.py:48
  174.4 464.0 %reduce-scatter.4.cloned.1.call-start = ((), (), s32[]{:S(2)}) async-start(), calls=%async_computation.7 | async-start | bytes 9437184 | tf_op jit(solution)/shard_map/reduce_scatter | solution.py:116
  174.4 116.7 %collective-permute-start.1 = (bf16[1,2048,768]{2,1,0:T(8,128)(2,1)}, bf16[1,2048,768]{2,1,0:T(8,128)(2,1)}, u32[]{:S(2)}, u32[]{:S(2)}) collective-permute-start(bf16[1,2048,768]{2,1,0:T(8,128)(2,1)} %param.16), channel_id=1, source_target_pairs={{0,32},{1,33},{2,34},{3,35},{4,36},{5,37},{6,38},{7,39},{8,40},{9,... | collective-permute-start | bytes 9437192 | tf_op jit(solution)/shard_map/ppermute | solution.py:8
  177.5 181.0 %collective-permute-start = (bf16[1,2048,768]{2,1,0:T(8,128)(2,1)}, bf16[1,2048,768]{2,1,0:T(8,128)(2,1)}, u32[]{:S(2)}, u32[]{:S(2)}) collective-permute-start(bf16[1,2048,768]{2,1,0:T(8,128)(2,1)} %param.15), channel_id=1, source_target_pairs={{0,32},{1,33},{2,34},{3,35},{4,36},{5,37},{6,38},{7,39},{8,40},{9,... | collective-permute-start | bytes 9437192 | tf_op jit(solution)/shard_map/ppermute | solution.py:8
  234.2 56.9 %copy-start.3 = (bf16[768,2048]{1,0:T(8,128)(2,1)S(1)}, bf16[768,2048]{1,0:T(8,128)(2,1)}, u32[]{:S(2)}) copy-start(bf16[768,2048]{1,0:T(8,128)(2,1)} %reshape.111) | copy-start | bytes 9437188
  365.3 1.0 copy-start.6
  370.9 271.2 %reduce-scatter.6.cloned.1.call-start = ((), (), s32[]{:S(2)}) async-start(), calls=%async_computation.8 | async-start | bytes 9437184 | tf_op jit(solution)/shard_map/reduce_scatter | solution.py:117
  378.5 341.7 %reduce-scatter.8.cloned.1.call-start = ((), (), s32[]{:S(2)}) async-start(), calls=%async_computation.9 | async-start | bytes 9437184 | tf_op jit(solution)/shard_map/reduce_scatter | solution.py:118
  392.3 26.6 %copy-start.5 = (bf16[768,768]{1,0:T(8,128)(2,1)S(1)}, bf16[768,768]{1,0:T(8,128)(2,1)}, u32[]{:S(2)}) copy-start(bf16[768,768]{1,0:T(8,128)(2,1)} %get-tuple-element.7) | copy-start | bytes 3538948
  392.3 124.9 %all-to-all-start.1 = ((bf16[64,12,2048]{2,1,0:T(8,128)(2,1)}), bf16[64,12,2048]{2,1,0:T(8,128)(2,1)}, u32[]{:S(2)}, u32[]{:S(2)}) async-start(bf16[64,12,2048]{2,1,0:T(8,128)(2,1)} %reshape.112), calls=%async_computation.1 | async-start | bytes 8388608 | tf_op jit(solution)/shard_map/all_to_all | solution.py:86
  418.9 4.4 copy-start.7
  517.2 100.3 %all-to-all-start.3 = ((bf16[64,12,2048]{2,1,0:T(8,128)(2,1)}), bf16[64,12,2048]{2,1,0:T(8,128)(2,1)}, u32[]{:S(2)}, u32[]{:S(2)}) async-start(bf16[64,12,2048]{2,1,0:T(8,128)(2,1)} %reshape.116), calls=%async_computation.3 | async-start | bytes 8388608 | tf_op jit(solution)/shard_map/all_to_all | solution.py:93
  642.2 82.0 %copy-start.1 = (bf16[128,2048]{1,0:T(8,128)(2,1)S(1)}, bf16[128,2048]{1,0:T(8,128)(2,1)}, u32[]{:S(2)}) copy-start(bf16[128,2048]{1,0:T(8,128)(2,1)} %param.10) | copy-start | bytes 1572868
Sparse Core Ops, SparseCore 0:
  371.1 141.4 reduce-scatter.3
  515.1 121.1 reduce-scatter.5
  638.7 81.4 reduce-scatter.7
where the time goes:
time: 740 us; the launch traced here: 731 us
  waiting for transfers between devices  436 us (59%)
  starting transfers between devices  126 us (17%)
  local copies, waits for them, and re-layouts  72 us (10%)
  matrix products  48 us (6%)
  other arithmetic  34.8 us (5%)
  between operations  15.1 us (2%)
    ppermute x3, waiting for transfers between devices, swapped(): lax.ppermute(array, axis, [(i, i ^ 1 << apart) for i in range(lax.axis_si...  115 us
    all_to_all x1, waiting for transfers between devices, body(): lax.all_to_all(expert_out.reshape(owner_count, capacity, width), 'expert'...  86.4 us
    all_to_all x1, waiting for transfers between devices, body(): lax.all_to_all(row_grad.reshape(owner_count, capacity, width), 'expert',...  81.7 us
    reduce_scatter x1, waiting for transfers between devices, body(): lax.psum_scatter(g_down, 'dp', scatter_dimension=0, tiled=True)  74.2 us
    all_to_all x1, starting transfers between devices, body(): lax.all_to_all(send_inputs.reshape(owner_count, capacity, width), 'expert...  74 us
    all_to_all x1, waiting for transfers between devices, body(): lax.all_to_all(send_inputs.reshape(owner_count, capacity, width), 'expert...  44.9 us
    all_to_all x1, waiting for transfers between devices, body(): lax.all_to_all(send_grads.reshape(owner_count, capacity, width), 'expert'...  33.2 us
    all_to_all x1, starting transfers between devices, body(): lax.all_to_all(expert_out.reshape(owner_count, capacity, width), 'expert'...  26.6 us
  transfers between devices with their start and end apart: 10, of which 7 were waited for; matrix products, arithmetic and copies ran while one was open for 15% of the time, Pallas kernels for 0%

commit v1 on v0

v1 whole, which is shorter than its diff:
```python
import jax
import jax.numpy as jnp
from jax import lax
from jax.experimental import pallas as pl
from jax.experimental.pallas import tpu as pltpu
from jax.sharding import PartitionSpec as P

MESH = pl.DeviceIdType.MESH
BF16 = jnp.bfloat16
F32 = jnp.float32
PLANE = 16
RINGS = 4
CAP = 12
ROWS = RINGS * CAP
TILE = 256
CONTRACT_ROWS = (((0,), (0,)), ((), ()))
CONTRACT_LAST = (((1,), (1,)), ((), ()))


def place():
    p = lax.axis_index("dp")
    e = lax.axis_index("expert")
    return p, lax.rem(e, PLANE), e // PLANE


def plane_peer(p, l, y, r):
    rc, rx, rz = r % 2, (r // 2) % 2, r // 4
    core, xh, z = lax.rem(l, 2), lax.rem(l // 2, 2), l // 4
    j = lax.rem(z + rz, 4) * 4 + lax.rem(xh + rx, 2) * 2 + lax.rem(core + rc, 2)
    return (p if rx == 0 else 1 - p, y * PLANE + j), j


def plane_source(p, l, y, r):
    rc, rx, rz = r % 2, (r // 2) % 2, r // 4
    core, xh, z = lax.rem(l, 2), lax.rem(l // 2, 2), l // 4
    j = lax.rem(z + 4 - rz, 4) * 4 + lax.rem(xh + rx, 2) * 2 + lax.rem(core + rc, 2)
    return (p if rx == 0 else 1 - p, y * PLANE + j), j


def ring_peer(p, l, y, d):
    return (p, lax.rem(y + d, RINGS) * PLANE + l)


def remote(src, dst, send, recv, device):
    return pltpu.make_async_remote_copy(
        src_ref=src, dst_ref=dst, send_sem=send, recv_sem=recv, device_id=device, device_id_type=MESH
    )


def greet(devices):
    barrier = pltpu.get_barrier_semaphore()
    for device in devices:
        pl.semaphore_signal(barrier, inc=1, device_id=device, device_id_type=MESH)
    return lambda: pl.semaphore_wait(barrier, len(devices))


def columns(n):
    return pl.ds(pl.multiple_of(n * TILE, TILE), TILE)


def selection(meta, base, ring):
    m = meta[ring]
    row = (lax.broadcasted_iota(jnp.int32, (PLANE * ROWS, 128), 0) + base).astype(F32)
    hit = jnp.zeros((PLANE * ROWS, 128), F32)
    weight = jnp.zeros((PLANE * ROWS, 128), F32)
    for k in range(4):
        same = row == m[k : k + 1, :]
        hit = jnp.where(same, 1.0, hit)
        weight = jnp.where(same, m[4 + k : 5 + k, :], weight)
    return hit, weight


def dispatch_kernel(
    ids, comb, plc, tok, cot, x_out, og_out, meta, gtok, gcot, pick, rw, sx, so,
    meta_send, meta_recv, ag_send, ag_recv, own_sem, d_send, d_recv,
):
    p, l, y = place()
    width = tok.shape[1]
    half = width // 2
    ring = [ring_peer(p, l, y, d) for d in range(1, RINGS)]
    peers = [plane_peer(p, l, y, r) for r in range(1, PLANE)]
    ready = greet(ring + [d for d, _ in peers])

    slots = plc.shape[0]
    tokens = ids.shape[1]
    slot_id = lax.broadcasted_iota(jnp.int32, (slots, tokens), 0)
    owned = [(plc[...] == ids[k : k + 1, :]) for k in range(4)]
    member = jnp.zeros((slots, tokens), F32)
    for o in owned:
        member = jnp.where(o, 1.0, member)
    before = (
        lax.broadcasted_iota(jnp.int32, (tokens, tokens), 0)
        < lax.broadcasted_iota(jnp.int32, (tokens, tokens), 1)
    ).astype(F32)
    rank = jnp.dot(member.astype(BF16), before.astype(BF16), preferred_element_type=F32)
    position = rank + (slot_id * ROWS + y * CAP).astype(F32)
    rows = [jnp.sum(jnp.where(o, position, 0.0), axis=0, keepdims=True) for o in owned]
    meta[y] = jnp.concatenate(rows + [comb[...]], axis=0)
    own_rows = pl.ds(pl.multiple_of(y * tokens, tokens), tokens)

    ready()
    copies = [
        remote(meta.at[y], meta.at[y], meta_send.at[d], meta_recv.at[d], ring[d]) for d in range(3)
    ]
    gather = []
    for c in range(4):
        src, dst = (tok, gtok) if c < 2 else (cot, gcot)
        cols = pl.ds((c % 2) * half, half)
        gather.append([
            remote(src.at[:, cols], dst.at[own_rows, cols], ag_send.at[c, d], ag_recv.at[c, d], ring[d])
            for d in range(3)
        ])
    for copy in copies + [g for group in gather for g in group]:
        copy.start()
    gtok[own_rows, :] = tok[...]
    gcot[own_rows, :] = cot[...]
    for copy in copies:
        copy.wait_recv()
    for b in range(RINGS):
        hit, weight = selection(meta, y * PLANE * ROWS, b)
        pick[:, b * tokens : (b + 1) * tokens] = hit.astype(BF16)
        total = jnp.sum(weight, axis=1, keepdims=True)
        rw[...] = total if b == 0 else rw[...] + total

    sent, locals_ = [], []
    for c in range(4):
        src, buf, dst = (gtok, sx, x_out) if c < 2 else (gcot, so, og_out)
        cols = pl.ds((c % 2) * half, half)
        for copy in gather[c]:
            copy.wait_recv()

        def step(n, _, src=src, buf=buf, c=c):
            at = columns((c % 2) * (half // TILE) + n)
            got = jnp.dot(pick[...], src[:, at], preferred_element_type=F32)
            if c >= 2:
                got = rw[...] * got
            buf[:, :, at] = got.astype(BF16).reshape(PLANE, ROWS, TILE)
            return 0

        lax.fori_loop(0, half // TILE, step, 0)
        for r, (device, j) in enumerate(peers):
            copy = remote(buf.at[j, :, cols], dst.at[l, :, cols], d_send.at[c, r], d_recv.at[c, r], device)
            copy.start()
            sent.append(copy)
        own = pltpu.make_async_copy(buf.at[l, :, cols], dst.at[l, :, cols], own_sem.at[c])
        own.start()
        locals_.append(own)
    for copy in sent:
        copy.wait()
    for copy in locals_:
        copy.wait()
    for copy in copies + [g for group in gather for g in group]:
        copy.wait_send()


def dispatch(ids, comb, plc, tok, cot):
    width = tok.shape[1]
    vmem = pl.BlockSpec(memory_space=pltpu.VMEM)
    hbm = pl.BlockSpec(memory_space=pl.ANY)
    row_shape = jax.ShapeDtypeStruct((PLANE, ROWS, width), BF16)
    dma = pltpu.SemaphoreType.DMA
    return pl.pallas_call(
        dispatch_kernel,
        name="dispatch",
        out_shape=(row_shape, row_shape, jax.ShapeDtypeStruct((RINGS, 8, 128), F32)),
        in_specs=[vmem] * 5,
        out_specs=(hbm, hbm, vmem),
        scratch_shapes=[
            pltpu.VMEM((512, width), BF16),
            pltpu.VMEM((512, width), BF16),
            pltpu.VMEM((PLANE * ROWS, 512), BF16),
            pltpu.VMEM((PLANE * ROWS, 1), F32),
            pltpu.VMEM((PLANE, ROWS, width), BF16),
            pltpu.VMEM((PLANE, ROWS, width), BF16),
            dma((3,)), dma((3,)), dma((4, 3)), dma((4, 3)), dma((4,)), dma((4, 15)), dma((4, 15)),
        ],
        compiler_params=pltpu.CompilerParams(
            collective_id=0, has_side_effects=True, vmem_limit_bytes=48 * 2**20
        ),
    )(ids, comb, plc, tok, cot)


def finish_kernel(
    eo, rg, meta, moved, g0, g1, g2, o0, o1, o2, mixed, input_grad, s0, s1, s2,
    ret, whi, wlo, pick, acc, part, own, gath,
    x0, x1, x2, y0, y1, y2, r0, r1, r2,
    x_send, x_recv, y_send, y_recv, own_sem, p_send, p_recv, b_send, b_recv,
):
    p, l, y = place()
    width = mixed.shape[1]
    tokens = mixed.shape[0]
    ring = [ring_peer(p, l, y, d) for d in range(1, RINGS)]
    peers = [plane_peer(p, l, y, r) for r in range(1, PLANE)]
    across = (1 - p, y * PLANE + l)
    ready = greet(ring + [d for d, _ in peers] + [across])
    grads = [(g0, o0, x0, y0, r0, s0), (g1, o1, x1, y1, r1, s1), (g2, o2, x2, y2, r2, s2)]

    ready()
    x_copies, y_copies = [], []
    sources = (eo, rg)
    back = [[], []]
    for which in range(2):
        for r, (device, j) in enumerate(peers):
            copy = remote(
                sources[which].at[j], ret.at[which, l], p_send.at[which, r], p_recv.at[which, r], device
            )
            back[which].append(copy)
        own_copy = pltpu.make_async_copy(sources[which].at[l], ret.at[which, l], own_sem.at[which])
        back[which].append(own_copy)
    for c in range(6):
        _, other, xr, _, _, _ = grads[c // 2]
        rows = other.shape[0] // 2
        at = pl.ds((c % 2) * rows, rows)
        x_copies.append(remote(other.at[at], xr.at[at], x_send.at[c], x_recv.at[c], across))
    for copy in back[0] + x_copies + back[1]:
        copy.start()
    for b in range(RINGS):
        hit, weight = selection(meta, y * PLANE * ROWS, b)
        cols = slice(b * tokens, (b + 1) * tokens)
        high = weight.astype(BF16)
        pick[:, cols] = hit.astype(BF16)
        whi[:, cols] = high
        wlo[:, cols] = (weight - high.astype(F32)).astype(BF16)

    own_rows = pl.ds(pl.multiple_of(y * tokens, tokens), tokens)
    summed = [[], []]

    def combine(which):
        for r, copy in enumerate(back[which]):
            if r < PLANE - 1:
                copy.wait_recv()
            else:
                copy.wait()

        def step(n, _):
            at = columns(n)
            rows = ret[which, :, :, at].reshape(PLANE * ROWS, TILE)
            if which == 0:
                total = lax.dot_general(whi[...], rows, CONTRACT_ROWS, preferred_element_type=F32)
                total += lax.dot_general(wlo[...], rows, CONTRACT_ROWS, preferred_element_type=F32)
            else:
                total = lax.dot_general(pick[...], rows, CONTRACT_ROWS, preferred_element_type=F32)
            acc[:, at] = total
            part[which, :, at] = total.astype(BF16)
            return 0

        lax.fori_loop(0, width // TILE, step, 0)
        own[which] = acc[own_rows, :]
        for d in range(3):
            there = pl.ds(pl.multiple_of(lax.rem(y + d + 1, RINGS) * tokens, tokens), tokens)
            copy = remote(
                part.at[which, there, :], gath.at[which, d], b_send.at[which, d], b_recv.at[which, d], ring[d]
            )
            copy.start()
            summed[which].append(copy)

    for c in range(6):
        mine, other, xr, ys, yr, _ = grads[c // 2]
        rows = other.shape[0] // 2
        at = pl.ds((c % 2) * rows, rows)
        x_copies[c].wait_recv()
        ys[at, :] = (0.5 * (mine[at, :] + xr[at, :].astype(F32))).astype(BF16)
        copy = remote(ys.at[at], yr.at[at], y_send.at[c], y_recv.at[c], ring[1])
        copy.start()
        y_copies.append(copy)
        if c == 1:
            combine(0)
        if c == 3:
            combine(1)
    for which, out in enumerate((mixed, input_grad)):
        total = own[which]
        for d in range(3):
            summed[which][d].wait_recv()
            total += gath[which, d].astype(F32)
        out[...] = total.astype(BF16)
    for c in range(6):
        _, other, _, ys, yr, out = grads[c // 2]
        rows = other.shape[0] // 2
        at = pl.ds((c % 2) * rows, rows)
        y_copies[c].wait_recv()
        out[at, :] = jnp.where(moved[0:1, 0:1] > 0.0, yr[at, :].astype(F32), ys[at, :].astype(F32)).astype(BF16)
    for copy in back[0][:-1] + back[1][:-1] + x_copies + y_copies + summed[0] + summed[1]:
        copy.wait_send()


def finish(eo, rg, meta, moved, own, other):
    width = eo.shape[-1]
    vmem = pl.BlockSpec(memory_space=pltpu.VMEM)
    hbm = pl.BlockSpec(memory_space=pl.ANY)
    dma = pltpu.SemaphoreType.DMA
    row_shape = jax.ShapeDtypeStruct((128, width), BF16)
    slabs = [pltpu.VMEM(o.shape, BF16) for o in other]
    return pl.pallas_call(
        finish_kernel,
        name="finish",
        out_shape=(row_shape, row_shape) + tuple(jax.ShapeDtypeStruct(o.shape, BF16) for o in other),
        in_specs=[hbm, hbm, vmem, vmem] + [vmem] * 3 + [hbm] * 3,
        out_specs=(vmem,) * 5,
        scratch_shapes=[
            pltpu.VMEM((2, PLANE, ROWS, width), BF16),
            pltpu.VMEM((PLANE * ROWS, 512), BF16),
            pltpu.VMEM((PLANE * ROWS, 512), BF16),
            pltpu.VMEM((PLANE * ROWS, 512), BF16),
            pltpu.VMEM((512, width), F32),
            pltpu.VMEM((2, 512, width), BF16),
            pltpu.VMEM((2, 128, width), F32),
            pltpu.VMEM((2, 3, 128, width), BF16),
        ]
        + slabs * 3
        + [dma((6,)), dma((6,)), dma((6,)), dma((6,)), dma((2,)), dma((2, 15)), dma((2, 15)), dma((2, 3)), dma((2, 3))],
        compiler_params=pltpu.CompilerParams(
            collective_id=1, has_side_effects=True, vmem_limit_bytes=62 * 2**20
        ),
    )(eo, rg, meta, moved, *own, *other)


def body(tokens, cotangent, expert_ids, combine, placement, moves, w_gate, w_up, w_down):
    gate_weight, up_weight, down_weight = w_gate[0], w_up[0], w_down[0]
    width, ff = gate_weight.shape
    p = lax.axis_index("dp")
    my_move = jnp.sum(jnp.where(jnp.arange(moves.shape[0]) == lax.axis_index("expert"), moves, 0))
    moved = jnp.broadcast_to(my_move.astype(F32), (8, 128))
    x, og, meta = dispatch(expert_ids.T, combine.T, placement[:, None], tokens, cotangent)
    row_inputs = x.reshape(PLANE * ROWS, width)
    out_grad = og.reshape(PLANE * ROWS, width)
    gate_pre = jnp.dot(row_inputs, gate_weight, preferred_element_type=F32)
    up_pre = jnp.dot(row_inputs, up_weight, preferred_element_type=F32)
    sigma = jax.nn.sigmoid(gate_pre)
    hidden = (gate_pre * sigma * up_pre).astype(BF16)
    expert_out = jnp.dot(hidden, down_weight, preferred_element_type=F32).astype(BF16)
    hidden_grad = lax.dot_general(out_grad, down_weight, CONTRACT_LAST, preferred_element_type=F32)
    gate_grad = (hidden_grad * up_pre * sigma * (1.0 + gate_pre * (1.0 - sigma))).astype(BF16)
    up_grad = (hidden_grad * gate_pre * sigma).astype(BF16)
    row_grad = (
        lax.dot_general(gate_grad, gate_weight, CONTRACT_LAST, preferred_element_type=F32)
        + lax.dot_general(up_grad, up_weight, CONTRACT_LAST, preferred_element_type=F32)
    ).astype(BF16)

    def halves(left, right):
        size = left.shape[1] // 2
        mine = lax.dynamic_slice_in_dim(left, p * size, size, 1)
        other = lax.dynamic_slice_in_dim(left, (1 - p) * size, size, 1)
        return (
            lax.dot_general(mine, right, CONTRACT_ROWS, preferred_element_type=F32),
            lax.dot_general(other, right, CONTRACT_ROWS, preferred_element_type=F32).astype(BF16),
        )

    pairs = [halves(row_inputs, gate_grad), halves(row_inputs, up_grad), halves(hidden, out_grad)]
    mixed, input_grad, *grads = finish(
        expert_out.reshape(PLANE, ROWS, width),
        row_grad.reshape(PLANE, ROWS, width),
        meta,
        moved,
        [a for a, _ in pairs],
        [b for _, b in pairs],
    )
    return (mixed, input_grad) + tuple(g.astype(F32)[None] for g in grads)


def solution(mesh):
    tok = P(("dp", "expert"), None)
    weight = P("expert", None, None)
    grad = P("expert", "dp", None)
    return jax.shard_map(
        body,
        mesh=mesh,
        in_specs=(tok, tok, tok, tok, P(), P(), weight, weight, weight),
        out_specs=(tok, tok, grad, grad, grad),
        check_vma=False,
    )
```

time: 740 us -> 336 us (0.45)
  waiting for transfers between devices: 436 us -> 0 us
  Pallas kernels: 0 us -> 272 us
  starting transfers between devices: 126 us -> 0 us
  local copies, waits for them, and re-layouts: 72 us -> 6.65 us
  other arithmetic: 34.8 us -> 7.86 us
  between operations: 15.1 us -> 1.43 us
    pallas_call x0 -> x2, Pallas kernels: none -> 272 us  [the longest x1 177 us: finish(): pl.pallas_call(finish_kernel, name='finish', out_shape=(row_shape, row_sh...]
    all_to_all x4 -> x0, waiting for transfers between devices: 246 us -> none  [the longest x1 86.4 us: body(): lax.all_to_all(expert_out.reshape(owner_count, capacity, width), 'expert'...]
    all_to_all x4 -> x0, starting transfers between devices: 119 us -> none  [the longest x1 74 us: body(): lax.all_to_all(send_inputs.reshape(owner_count, capacity, width), 'expert...]
    ppermute x3 -> x0, waiting for transfers between devices: 115 us -> none  [swapped(): lax.ppermute(array, axis, [(i, i ^ 1 << apart) for i in range(lax.axis_si...]
    reduce_scatter x3 -> x0, waiting for transfers between devices: 74.2 us -> none  [the longest x1 74.2 us: body(): lax.psum_scatter(g_down, 'dp', scatter_dimension=0, tiled=True)]
    reshape x8 -> x0, local copies, waits for them, and re-layouts: 29 us -> none  [the longest x1 6.15 us: body(): row_inputs = arrived[0].reshape(buffer_rows, width)]
    gather x5 -> x0, local copies, waits for them, and re-layouts: 21.1 us -> none  [the longest x2 10.3 us: body(): tokens[source_row]]
    convert_element_type x2 -> x0, local copies, waits for them, and re-layouts: 11.2 us -> none  [the longest x1 6.46 us: body(): cotangent[source_row].astype(jnp.float32)]
  transfers between devices with their start and end apart: 10 -> 0, of which waited for: 7 -> 0; matrix products, arithmetic and copies ran while one was open for 15% -> 0% of each run, Pallas kernels for 0% -> 0%
where the time goes in v1:
time: 336 us; the launch traced here: 333 us
  Pallas kernels  272 us (81%)
  matrix products  44.8 us (13%)
  other arithmetic  7.86 us (2%)
  local copies, waits for them, and re-layouts  6.65 us (2%)
    pallas_call x1, Pallas kernels, finish(): pl.pallas_call(finish_kernel, name='finish', out_shape=(row_shape, row_sh...  177 us
    pallas_call x1, Pallas kernels, dispatch(): pl.pallas_call(dispatch_kernel, name='dispatch', out_shape=(row_shape, ro...  95.1 us
    dot_general x3, matrix products, halves(): lax.dot_general(mine, right, CONTRACT_ROWS, preferred_element_type=F32)  11.9 us
    dot_general x3, matrix products, halves(): lax.dot_general(other, right, CONTRACT_ROWS, preferred_element_type=F32)  10.3 us
    broadcast_in_dim x2, other arithmetic, body(): return (mixed, input_grad) + tuple((g.astype(F32)[None] for g in grads))  7.23 us

profile of v1, /device:TPU:1, one launch (start us, length us, event | category | flops | bytes accessed | tf_op | source)
XLA Modules:
  0.0 333.2 jit_solution(7613702540470602396)
XLA Ops:
  0.6 0.7 copy.14.plc
  1.4 0.0 copy-start
  1.4 1.0 copy-done
  2.4 1.0 copy-done.1
  3.5 0.7 copy-done.3
  4.1 0.7 copy-done.4
  4.8 95.1 %dispatch.1 = (bf16[16,48,2048]{2,1,0:T(8,128)(2,1)S(1)}, bf16[16,48,2048]{2,1,0:T(8,128)(2,1)}, f32[4,8,128]{2,1,0:T(8,128)S(1)}) custom-call(s32[4,128]{1,0:T(4,128)S(1)} %bitcast.45, f32[4,128]{1,0:T(4,128)S(1)} %bitcast.46, s32[64,1]{1,0:T(8,128)S(1)} %copy.14.plc, bf16[128,2048]{1,0:T(8,128)(2,1)S(1)} %copy-done, bf16[128,2048]{1,0:T(8,128)(2,1)S(1)} %copy-done.1), custom_call_target="tpu_custom_call" | custom-call | tf_op jit(solution)/shard_map/dispatch/pallas_call | solution.py:162
  100.0 0.0 copy-start.2
  100.0 0.0 copy-start.11
  100.0 4.6 %fusion.4 = f32[768,768]{1,0:T(8,128)S(1)} fusion(bf16[768,2048]{1,0:T(8,128)(2,1)S(1)} %bitcast.47, bf16[1,2048,768]{2,1,0:T(8,128)(2,1)} %param.16), kind=kOutput, calls=%fused_computation.6 | convolution fusion | flops 2415919104 | bytes 8650752 | tf_op jit(solution)/shard_map/dot_general | solution.py:327
  104.6 0.0 copy-done.2
  104.6 0.0 copy-done.11
  104.7 0.0 copy-start.5
  104.7 0.0 copy-start.14
  104.7 2.6 fusion.8
  107.3 0.0 copy-done.5
  107.3 0.2 copy-done.14
  107.5 4.9 %multiply_convert_fusion = (bf16[768,768]{1,0:T(8,128)(2,1)}, bf16[768,768]{1,0:T(8,128)(2,1)}, bf16[768,768]{1,0:T(8,128)(2,1)}) fusion(f32[768,768]{1,0:T(8,128)S(1)} %fusion.8, f32[768,768]{1,0:T(8,128)S(1)} %fusion.4, bf16[768,2048]{1,0:T(8,128)(2,1)S(1)} %bitcast.55, bf16[1,768,2048]{2,1,0:T(8,128)(2,1)S(1)} %copy-done.14), kind=kOutput, calls=%fused_computation.13 | convolution fusion | flops 2425356288 | bytes 14548992 | tf_op jit(solution)/shard_map/dot_general | solution.py:331
  112.4 4.1 %convolution_convert_fusion.2.o1 = bf16[1024,768]{1,0:T(8,128)(2,1)} fusion(bf16[768,768]{1,0:T(8,128)(2,1)} %get-tuple-element.21, bf16[768,2048]{1,0:T(8,128)(2,1)S(1)} %bitcast.49, s32[]{:T(128)S(6)} %select_n.21), kind=kOutput, calls=%fused_computation.17 | convolution fusion | flops 1208745984 | bytes 4325380 | tf_op jit(solution)/shard_map/dot_general | solution.py:345
  116.4 0.0 copy-done.18
  116.4 2.6 convolution_convert_fusion.3.o0
  119.0 4.4 %fusion.12.g1 = f32[1024,768]{1,0:T(8,128)} fusion(bf16[768,768]{1,0:T(8,128)(2,1)} %get-tuple-element.21, bf16[768,2048]{1,0:T(8,128)(2,1)S(1)} %bitcast.51, s32[]{:T(128)S(6)} %select_n.19), kind=kOutput, calls=%fused_computation.24 | convolution fusion | flops 1207959552 | bytes 5898244 | tf_op jit(solution)/shard_map/dot_general | solution.py:344
  123.5 0.0 copy-done.19
  123.5 3.1 fusion.14.g0
  126.6 0.0 copy-done.12
  126.6 2.6 fusion.6
  129.2 0.0 copy-done.13
  129.3 0.0 copy-done.17
  129.3 0.0 copy-start.6
  129.3 4.0 %add_convert_fusion = bf16[768,2048]{1,0:T(8,128)(2,1)} fusion(f32[768,2048]{1,0:T(8,128)S(1)} %fusion.6, bf16[768,768]{1,0:T(8,128)(2,1)S(1)} %copy-done.17, bf16[1,2048,768]{2,1,0:T(8,128)(2,1)S(1)} %copy-done.13), kind=kOutput, calls=%fused_computation | convolution fusion | flops 2419064832 | bytes 13762560 | tf_op jit(solution)/shard_map/dot_general | solution.py:336
  133.3 0.0 copy-done.6
  133.3 3.6 %convolution_convert_fusion.1.o2 = bf16[384,2048]{1,0:T(8,128)(2,1)} fusion(bf16[768,2048]{1,0:T(8,128)(2,1)S(1)} %bitcast.56, bf16[768,768]{1,0:T(8,128)(2,1)} %get-tuple-element.23, s32[]{:T(128)S(6)} %select_n.22), kind=kOutput, calls=%fused_computation.12 | convolution fusion | flops 1208745984 | bytes 5308420 | tf_op jit(solution)/shard_map/dot_general | solution.py:345
  136.9 4.3 %fusion.17.g2 = f32[384,2048]{1,0:T(8,128)} fusion(bf16[768,2048]{1,0:T(8,128)(2,1)S(1)} %bitcast.57, bf16[768,768]{1,0:T(8,128)(2,1)} %get-tuple-element.23, s32[]{:T(128)S(6)} %select_n.20), kind=kOutput, calls=%fused_computation.29 | convolution fusion | flops 1207959552 | bytes 6881284 | tf_op jit(solution)/shard_map/dot_general | solution.py:344
  141.2 0.0 copy-done.10
  141.2 0.0 copy-done.15
  141.2 3.9 %convolution_convert_fusion = bf16[768,2048]{1,0:T(8,128)(2,1)} fusion(bf16[768,768]{1,0:T(8,128)(2,1)S(1)} %copy-done.10, bf16[1,768,2048]{2,1,0:T(8,128)(2,1)S(1)} %copy-done.15), kind=kOutput, calls=%fused_computation.1 | convolution fusion | flops 2417491968 | bytes 7471104 | tf_op jit(solution)/shard_map/dot_general | solution.py:330
  145.2 0.0 copy-done.16
  145.2 0.6 fusion.25
  146.5 0.6 broadcast_in_dim.30.moved
  147.1 177.3 %finish.1 = (bf16[128,2048]{1,0:T(8,128)(2,1)}, bf16[128,2048]{1,0:T(8,128)(2,1)}, bf16[1024,768]{1,0:T(8,128)(2,1)}, bf16[1024,768]{1,0:T(8,128)(2,1)}, bf16[384,2048]{1,0:T(8,128)(2,1)}) custom-call(bf16[16,48,2048]{2,1,0:T(8,128)(2,1)} %bitcast.54, bf16[16,48,2048]{2,1,0:T(8,128)(2,1)} %bitcast.53, f32[4,8,128]{2,1,0:T(8,128)} %copy-done.2, ...), custom_call_target="tpu_custom_call" | custom-call | tf_op jit(solution)/shard_map/finish/pallas_call | solution.py:293
  324.4 0.0 copy-start.7
  324.4 5.2 %bitcast_convert_fusion.1 = (f32[1,1024,768]{2,1,0:T(8,128)}, f32[1,1024,768]{2,1,0:T(8,128)}) fusion(bf16[1024,768]{1,0:T(8,128)(2,1)} %get-tuple-element.19, bf16[1024,768]{1,0:T(8,128)(2,1)} %get-tuple-element.18), kind=kLoop, calls=%fused_computation.20 | loop fusion | flops 1572864 | bytes 9437184 | tf_op jit(solution)/shard_map/broadcast_in_dim | solution.py:357
  329.5 0.0 copy-done.7
  329.6 2.0 bitcast_convert_fusion
  331.6 0.0 copy-done.9
  331.6 0.8 copy.17
  332.4 0.0 copy-done.8
  332.4 0.8 copy.18
  (13 shorter events, 0.0 us)
Async XLA Ops:
  1.4 1.0 copy-start
  2.4 1.0 copy-start.1
  3.5 0.7 copy-start.3
  4.1 0.7 copy-start.4
  100.0 4.7 %copy-start.2 = (f32[4,8,128]{2,1,0:T(8,128)}, f32[4,8,128]{2,1,0:T(8,128)S(1)}, u32[]{:S(2)}) copy-start(f32[4,8,128]{2,1,0:T(8,128)S(1)} %get-tuple-element.15.meta) | copy-start | bytes 49156
  100.0 4.7 %copy-start.11 = (bf16[1,2048,768]{2,1,0:T(8,128)(2,1)S(1)}, bf16[1,2048,768]{2,1,0:T(8,128)(2,1)}, u32[]{:S(2)}) copy-start(bf16[1,2048,768]{2,1,0:T(8,128)(2,1)} %param.15) | copy-start | bytes 9437188
  104.7 2.6 copy-start.5
  104.7 2.8 copy-start.14
  112.4 4.1 %copy-start.18 = (bf16[768,768]{1,0:T(8,128)(2,1)S(1)}, bf16[768,768]{1,0:T(8,128)(2,1)}, u32[]{:S(2)}) copy-start(bf16[768,768]{1,0:T(8,128)(2,1)} %get-tuple-element.22) | copy-start | bytes 3538948
  119.0 4.5 %copy-start.19 = (bf16[768,768]{1,0:T(8,128)(2,1)S(1)}, bf16[768,768]{1,0:T(8,128)(2,1)}, u32[]{:S(2)}) copy-start(bf16[768,768]{1,0:T(8,128)(2,1)} %get-tuple-element.22) | copy-start | bytes 3538948
  123.5 3.1 copy-start.12
  126.6 2.6 copy-start.13
  126.6 2.6 copy-start.17
  129.3 4.0 %copy-start.6 = (bf16[16,48,2048]{2,1,0:T(8,128)(2,1)S(1)}, bf16[16,48,2048]{2,1,0:T(8,128)(2,1)}, u32[]{:S(2)}) copy-start(bf16[16,48,2048]{2,1,0:T(8,128)(2,1)} %get-tuple-element.14) | copy-start | bytes 9437188
  136.9 4.3 %copy-start.10 = (bf16[768,768]{1,0:T(8,128)(2,1)S(1)}, bf16[768,768]{1,0:T(8,128)(2,1)}, u32[]{:S(2)}) copy-start(bf16[768,768]{1,0:T(8,128)(2,1)} %get-tuple-element.23) | copy-start | bytes 3538948
  136.9 4.3 %copy-start.15 = (bf16[1,768,2048]{2,1,0:T(8,128)(2,1)S(1)}, bf16[1,768,2048]{2,1,0:T(8,128)(2,1)}, u32[]{:S(2)}) copy-start(bf16[1,768,2048]{2,1,0:T(8,128)(2,1)} %param.17) | copy-start | bytes 9437188
  141.2 4.0 %copy-start.16 = (s32[64]{0:T(128)S(1)}, s32[64]{0:T(128)}, u32[]{:S(2)}) copy-start(s32[64]{0:T(128)} %param.14) | copy-start | bytes 772
  324.4 5.2 %copy-start.7 = (bf16[384,2048]{1,0:T(8,128)(2,1)S(1)}, bf16[384,2048]{1,0:T(8,128)(2,1)}, u32[]{:S(2)}) copy-start(bf16[384,2048]{1,0:T(8,128)(2,1)} %get-tuple-element.20) | copy-start | bytes 4718596
  329.6 2.1 copy-start.9
  329.6 2.8 copy-start.8

commit v2 on v1

v2 whole, which is shorter than its diff:
```python
import jax
import jax.numpy as jnp
from jax import lax
from jax.experimental import pallas as pl
from jax.experimental.pallas import tpu as pltpu
from jax.sharding import PartitionSpec as P

MESH = pl.DeviceIdType.MESH
BF16 = jnp.bfloat16
F32 = jnp.float32
PLANE = 16
RINGS = 4
CAP = 12
ROWS = RINGS * CAP
TILE = 256
CONTRACT_ROWS = (((0,), (0,)), ((), ()))
CONTRACT_LAST = (((1,), (1,)), ((), ()))


def place():
    p = lax.axis_index("dp")
    e = lax.axis_index("expert")
    return p, lax.rem(e, PLANE), e // PLANE


def plane_peer(p, l, y, r):
    rc, rx, rz = r % 2, (r // 2) % 2, r // 4
    core, xh, z = lax.rem(l, 2), lax.rem(l // 2, 2), l // 4
    j = lax.rem(z + rz, 4) * 4 + lax.rem(xh + rx, 2) * 2 + lax.rem(core + rc, 2)
    return (p if rx == 0 else 1 - p, y * PLANE + j), j


def plane_source(p, l, y, r):
    rc, rx, rz = r % 2, (r // 2) % 2, r // 4
    core, xh, z = lax.rem(l, 2), lax.rem(l // 2, 2), l // 4
    j = lax.rem(z + 4 - rz, 4) * 4 + lax.rem(xh + rx, 2) * 2 + lax.rem(core + rc, 2)
    return (p if rx == 0 else 1 - p, y * PLANE + j), j


def ring_peer(p, l, y, d):
    return (p, lax.rem(y + d, RINGS) * PLANE + l)


def remote(src, dst, send, recv, device):
    return pltpu.make_async_remote_copy(
        src_ref=src, dst_ref=dst, send_sem=send, recv_sem=recv, device_id=device, device_id_type=MESH
    )


def greet(devices):
    barrier = pltpu.get_barrier_semaphore()
    for device in devices:
        pl.semaphore_signal(barrier, inc=1, device_id=device, device_id_type=MESH)
    return lambda: pl.semaphore_wait(barrier, len(devices))


def columns(n):
    return pl.ds(pl.multiple_of(n * TILE, TILE), TILE)


def selection(meta, base, ring):
    m = meta[ring]
    row = (lax.broadcasted_iota(jnp.int32, (PLANE * ROWS, 128), 0) + base).astype(F32)
    hit = jnp.zeros((PLANE * ROWS, 128), F32)
    weight = jnp.zeros((PLANE * ROWS, 128), F32)
    for k in range(4):
        same = row == m[k : k + 1, :]
        hit = jnp.where(same, 1.0, hit)
        weight = jnp.where(same, m[4 + k : 5 + k, :], weight)
    return hit, weight


def load(src, dst, sem):
    copy = pltpu.make_async_copy(src, dst, sem)
    copy.start()
    return copy


def dispatch_kernel(
    ids, comb, plc, tok, cot, wg, wu, wd, x_out, og_out, meta, pre_out, hid_out, eo_out,
    gtok, gcot, pick, rw, sx, so, x, wgu, wdv, pre, hid, eo,
    meta_send, meta_recv, ag_send, ag_recv, own_sem, d_send, d_recv, w_sem, out_sem,
):
    p, l, y = place()
    width = tok.shape[1]
    ff = wg.shape[1]
    half = width // 2
    ring = [ring_peer(p, l, y, d) for d in range(1, RINGS)]
    peers = [plane_peer(p, l, y, r) for r in range(1, PLANE)]
    ready = greet(ring + [d for d, _ in peers])
    weights = [
        load(wg, wgu.at[:, pl.ds(0, ff)], w_sem.at[0]),
        load(wu, wgu.at[:, pl.ds(ff, ff)], w_sem.at[1]),
        load(wd, wdv, w_sem.at[2]),
    ]

    slots = plc.shape[0]
    tokens = ids.shape[1]
    slot_id = lax.broadcasted_iota(jnp.int32, (slots, tokens), 0)
    owned = [(plc[...] == ids[k : k + 1, :]) for k in range(4)]
    member = jnp.zeros((slots, tokens), F32)
    for o in owned:
        member = jnp.where(o, 1.0, member)
    before = (
        lax.broadcasted_iota(jnp.int32, (tokens, tokens), 0)
        < lax.broadcasted_iota(jnp.int32, (tokens, tokens), 1)
    ).astype(F32)
    rank = jnp.dot(member.astype(BF16), before.astype(BF16), preferred_element_type=F32)
    position = rank + (slot_id * ROWS + y * CAP).astype(F32)
    rows = [jnp.sum(jnp.where(o, position, 0.0), axis=0, keepdims=True) for o in owned]
    meta[y] = jnp.concatenate(rows + [comb[...]], axis=0)
    own_rows = pl.ds(pl.multiple_of(y * tokens, tokens), tokens)

    ready()
    copies = [
        remote(meta.at[y], meta.at[y], meta_send.at[d], meta_recv.at[d], ring[d]) for d in range(3)
    ]
    gather = []
    for c in range(4):
        src, dst = (tok, gtok) if c < 2 else (cot, gcot)
        cols = pl.ds((c % 2) * half, half)
        gather.append([
            remote(src.at[:, cols], dst.at[own_rows, cols], ag_send.at[c, d], ag_recv.at[c, d], ring[d])
            for d in range(3)
        ])
    for copy in copies + [g for group in gather for g in group]:
        copy.start()
    gtok[own_rows, :] = tok[...]
    gcot[own_rows, :] = cot[...]
    for copy in copies:
        copy.wait_recv()
    for b in range(RINGS):
        hit, weight = selection(meta, y * PLANE * ROWS, b)
        pick[:, b * tokens : (b + 1) * tokens] = hit.astype(BF16)
        total = jnp.sum(weight, axis=1, keepdims=True)
        rw[...] = total if b == 0 else rw[...] + total

    sent, own = [], []
    for c in range(4):
        src, buf, dst = (gtok, sx, x) if c < 2 else (gcot, so, og_out)
        cols = pl.ds((c % 2) * half, half)
        for copy in gather[c]:
            copy.wait_recv()

        def step(n, _, src=src, buf=buf, c=c):
            at = columns((c % 2) * (half // TILE) + n)
            got = jnp.dot(pick[...], src[:, at], preferred_element_type=F32)
            if c >= 2:
                got = rw[...] * got
            buf[:, :, at] = got.astype(BF16).reshape(PLANE, ROWS, TILE)
            return 0

        lax.fori_loop(0, half // TILE, step, 0)
        group = []
        for r, (device, j) in enumerate(peers):
            copy = remote(buf.at[j, :, cols], dst.at[l, :, cols], d_send.at[c, r], d_recv.at[c, r], device)
            copy.start()
            group.append(copy)
        sent.append(group)
        own.append(load(buf.at[l, :, cols], dst.at[l, :, cols], own_sem.at[c]))

    for c in range(2):
        own[c].wait()
        for copy in sent[c]:
            copy.wait_recv()
    outs = [load(x, x_out, out_sem.at[0])]
    for copy in weights:
        copy.wait()

    def forward(n, _):
        gate_at = columns(n)
        up_at = columns(ff // TILE + n)
        rows = x[...].reshape(PLANE * ROWS, width)
        gate = jnp.dot(rows, wgu[:, gate_at], preferred_element_type=F32)
        up = jnp.dot(rows, wgu[:, up_at], preferred_element_type=F32)
        pre[:, gate_at] = gate
        pre[:, up_at] = up
        hid[:, gate_at] = (gate * jax.nn.sigmoid(gate) * up).astype(BF16)
        return 0

    lax.fori_loop(0, ff // TILE, forward, 0)
    outs.append(load(pre, pre_out, out_sem.at[1]))
    outs.append(load(hid, hid_out, out_sem.at[2]))

    def project(n, _):
        at = columns(n)
        got = jnp.dot(hid[...], wdv[:, at], preferred_element_type=F32)
        eo[:, :, at] = got.astype(BF16).reshape(PLANE, ROWS, TILE)
        return 0

    lax.fori_loop(0, width // TILE, project, 0)
    outs.append(load(eo, eo_out, out_sem.at[3]))
    for c in range(2, 4):
        own[c].wait()
        for copy in sent[c]:
            copy.wait_recv()
    for copy in outs:
        copy.wait()
    for copy in copies + [g for group in gather + sent for g in group]:
        copy.wait_send()


def dispatch(ids, comb, plc, tok, cot, wg, wu, wd):
    width = tok.shape[1]
    ff = wg.shape[1]
    rows = PLANE * ROWS
    vmem = pl.BlockSpec(memory_space=pltpu.VMEM)
    hbm = pl.BlockSpec(memory_space=pl.ANY)
    row_shape = jax.ShapeDtypeStruct((PLANE, ROWS, width), BF16)
    row_buffer = pltpu.VMEM((PLANE, ROWS, width), BF16)
    dma = pltpu.SemaphoreType.DMA
    return pl.pallas_call(
        dispatch_kernel,
        name="dispatch",
        out_shape=(
            row_shape,
            row_shape,
            jax.ShapeDtypeStruct((RINGS, 8, 128), F32),
            jax.ShapeDtypeStruct((rows, 2 * ff), F32),
            jax.ShapeDtypeStruct((rows, ff), BF16),
            row_shape,
        ),
        in_specs=[vmem] * 5 + [hbm] * 3,
        out_specs=(hbm, hbm, vmem, hbm, hbm, hbm),
        scratch_shapes=[
            pltpu.VMEM((512, width), BF16),
            pltpu.VMEM((512, width), BF16),
            pltpu.VMEM((rows, 512), BF16),
            pltpu.VMEM((rows, 1), F32),
            row_buffer,
            row_buffer,
            row_buffer,
            pltpu.VMEM((width, 2 * ff), BF16),
            pltpu.VMEM((ff, width), BF16),
            pltpu.VMEM((rows, 2 * ff), F32),
            pltpu.VMEM((rows, ff), BF16),
            row_buffer,
            dma((3,)), dma((3,)), dma((4, 3)), dma((4, 3)), dma((4,)), dma((4, 15)), dma((4, 15)),
            dma((3,)), dma((4,)),
        ],
        compiler_params=pltpu.CompilerParams(
            collective_id=0, has_side_effects=True, vmem_limit_bytes=60 * 2**20
        ),
    )(ids, comb, plc, tok, cot, wg, wu, wd)


DOWN = 128
WIDE = 256
NARROW = 128


def finish_kernel(
    x_in, og_in, eo, pre_in, hid_in, meta, wg, wu, wd,
    mixed, input_grad, own_down, own_wide, got_down, got_wide,
    x, og, pre, hid, wgu, wdv, gu, rg, ret, whi, wlo, pick, acc, part, own, gath, fresh,
    oth_down, oth_wide, x_down, x_wide,
    in_sem, x_send, x_recv, y_send, y_recv, s_sem, own_sem, p_send, p_recv, b_send, b_recv,
):
    p, l, y = place()
    tokens, width = mixed.shape
    ff = hid.shape[1]
    rows_all = PLANE * ROWS
    ring = [ring_peer(p, l, y, d) for d in range(1, RINGS)]
    peers = [plane_peer(p, l, y, r) for r in range(1, PLANE)]
    across = (1 - p, y * PLANE + l)
    ready = greet(ring + [d for d, _ in peers] + [across])
    loads = [
        load(hid_in, hid, in_sem.at[0]),
        load(og_in, og, in_sem.at[1]),
        load(wd, wdv, in_sem.at[2]),
        load(pre_in, pre, in_sem.at[3]),
        load(x_in, x, in_sem.at[4]),
        load(wg, wgu.at[:, pl.ds(0, ff)], in_sem.at[5]),
        load(wu, wgu.at[:, pl.ds(ff, ff)], in_sem.at[6]),
    ]
    downs = (ff // 2) // DOWN
    narrows = (width // 2) // NARROW
    chunks = downs + narrows

    def slab(c, down, wide):
        if c < downs:
            return down.at[pl.ds(c * DOWN, DOWN)]
        return wide.at[pl.ds((c - downs) * NARROW, NARROW)]

    def down_part(side, c):
        at = pl.ds(pl.multiple_of(side * (ff // 2) + c * DOWN, DOWN), DOWN)
        return lambda cols: lax.dot_general(
            hid[:, at], og[:, :, cols].reshape(rows_all, -1), CONTRACT_ROWS, preferred_element_type=F32
        )

    def wide_part(side, c):
        at = pl.ds(pl.multiple_of(side * (width // 2) + c * WIDE, WIDE), WIDE)
        return lambda cols: lax.dot_general(
            x[:, :, at].reshape(rows_all, WIDE), gu[:, cols], CONTRACT_ROWS, preferred_element_type=F32
        )

    back = [[], []]
    for which, source in enumerate((eo, rg)):
        for r, (device, j) in enumerate(peers):
            back[which].append(
                remote(source.at[j], ret.at[which, l], p_send.at[which, r], p_recv.at[which, r], device)
            )
        back[which].append(pltpu.make_async_copy(source.at[l], ret.at[which, l], own_sem.at[which]))
    x_copies = [
        remote(slab(c, oth_down, oth_wide), slab(c, x_down, x_wide), x_send.at[c], x_recv.at[c], across)
        for c in range(chunks)
    ]
    y_copies = [
        remote(slab(c, x_down, x_wide), slab(c, got_down, got_wide), y_send.at[c], y_recv.at[c], ring[1])
        for c in range(chunks)
    ]
    kept = [
        pltpu.make_async_copy(slab(c, x_down, x_wide), slab(c, own_down, own_wide), s_sem.at[c])
        for c in range(chunks)
    ]

    ready()
    loads[0].wait()
    loads[1].wait()
    for c in range(downs):
        part_of = down_part(1 - p, c)
        for n in range(width // 512):
            cols = slice(n * 512, (n + 1) * 512)
            oth_down[c * DOWN : (c + 1) * DOWN, cols] = (0.5 * part_of(cols)).astype(BF16)
        x_copies[c].start()
        if c == 0:
            for copy in back[0]:
                copy.start()
    loads[2].wait()
    loads[3].wait()

    def backward(n, _):
        gate_at = columns(n)
        up_at = columns(ff // TILE + n)
        grad = lax.dot_general(
            og[...].reshape(rows_all, width), wdv[gate_at, :], CONTRACT_LAST, preferred_element_type=F32
        )
        gate, up = pre[:, gate_at], pre[:, up_at]
        sigma = jax.nn.sigmoid(gate)
        gu[:, gate_at] = (grad * up * sigma * (1.0 + gate * (1.0 - sigma))).astype(BF16)
        gu[:, up_at] = (grad * gate * sigma).astype(BF16)
        return 0

    lax.fori_loop(0, ff // TILE, backward, 0)
    loads[4].wait()
    per = WIDE // NARROW
    for c in range(narrows // per):
        part_of = wide_part(1 - p, c)
        for n in range(2):
            cols = slice(n * ff, (n + 1) * ff)
            oth_wide[c * WIDE : (c + 1) * WIDE, cols] = (0.5 * part_of(cols)).astype(BF16)
        for i in range(per):
            x_copies[downs + c * per + i].start()
    loads[5].wait()
    loads[6].wait()

    def pull(n, _):
        at = columns(n)
        got = lax.dot_general(gu[...], wgu[at, :], CONTRACT_LAST, preferred_element_type=F32)
        rg[:, :, at] = got.astype(BF16).reshape(PLANE, ROWS, TILE)
        return 0

    lax.fori_loop(0, width // TILE, pull, 0)
    for copy in back[1]:
        copy.start()
    for b in range(RINGS):
        hit, weight = selection(meta, y * PLANE * ROWS, b)
        cols = slice(b * tokens, (b + 1) * tokens)
        high = weight.astype(BF16)
        pick[:, cols] = hit.astype(BF16)
        whi[:, cols] = high
        wlo[:, cols] = (weight - high.astype(F32)).astype(BF16)

    own_rows = pl.ds(pl.multiple_of(y * tokens, tokens), tokens)
    summed = [[], []]

    def combine(which):
        for copy in back[which][:-1]:
            copy.wait_recv()
        back[which][-1].wait()

        def step(n, _):
            at = columns(n)
            rows = ret[which, :, :, at].reshape(rows_all, TILE)
            if which == 0:
                total = lax.dot_general(whi[...], rows, CONTRACT_ROWS, preferred_element_type=F32)
                total += lax.dot_general(wlo[...], rows, CONTRACT_ROWS, preferred_element_type=F32)
            else:
                total = lax.dot_general(pick[...], rows, CONTRACT_ROWS, preferred_element_type=F32)
            acc[...] = total
            part[which, :, at] = total.astype(BF16)
            own[which, :, at] = acc[own_rows, :]
            return 0

        lax.fori_loop(0, width // TILE, step, 0)
        for d in range(3):
            there = pl.ds(pl.multiple_of(lax.rem(y + d + 1, RINGS) * tokens, tokens), tokens)
            copy = remote(
                part.at[which, there, :], gath.at[which, d], b_send.at[which, d], b_recv.at[which, d], ring[d]
            )
            copy.start()
            summed[which].append(copy)

    for c in range(chunks):
        if c < downs:
            part_of = down_part(p, c)
            at = slice(c * DOWN, (c + 1) * DOWN)
            x_copies[c].wait_recv()
            for n in range(width // 512):
                cols = slice(n * 512, (n + 1) * 512)
                x_down[at, cols] = (0.5 * part_of(cols) + x_down[at, cols].astype(F32)).astype(BF16)
        else:
            i = c - downs
            if i % per == 0:
                part_of = wide_part(p, i // per)
                for n in range(2):
                    cols = slice(n * ff, (n + 1) * ff)
                    fresh[:, cols] = 0.5 * part_of(cols)
            at = slice(i * NARROW, (i + 1) * NARROW)
            x_copies[c].wait_recv()
            mine = fresh[(i % per) * NARROW : (i % per + 1) * NARROW, :]
            x_wide[at, :] = (mine + x_wide[at, :].astype(F32)).astype(BF16)
        y_copies[c].start()
        kept[c].start()
        if c == EARLY:
            combine(0)
        if c == LATE:
            combine(1)
    for which, out in enumerate((mixed, input_grad)):
        total = own[which]
        for d in range(3):
            summed[which][d].wait_recv()
            total += gath[which, d].astype(F32)
        out[...] = total.astype(BF16)
    for c in range(chunks):
        y_copies[c].wait()
        kept[c].wait()
    for copy in back[0][:-1] + back[1][:-1] + x_copies + summed[0] + summed[1]:
        copy.wait_send()


EARLY = 2
LATE = 7


def finish(x, og, eo, pre, hid, meta, wg, wu, wd):
    width = x.shape[-1]
    ff = hid.shape[1]
    rows = PLANE * ROWS
    vmem = pl.BlockSpec(memory_space=pltpu.VMEM)
    hbm = pl.BlockSpec(memory_space=pl.ANY)
    dma = pltpu.SemaphoreType.DMA
    chunks = (ff // 2) // DOWN + (width // 2) // NARROW
    row_shape = jax.ShapeDtypeStruct((128, width), BF16)
    row_buffer = pltpu.VMEM((PLANE, ROWS, width), BF16)
    down_shape, wide_shape = (ff // 2, width), (width // 2, 2 * ff)
    grads = [jax.ShapeDtypeStruct(s, BF16) for s in (down_shape, wide_shape)]
    slabs = [pltpu.VMEM(s, BF16) for s in (down_shape, wide_shape)]
    return pl.pallas_call(
        finish_kernel,
        name="finish",
        out_shape=(row_shape, row_shape, *grads, *grads),
        in_specs=[hbm] * 5 + [vmem] + [hbm] * 3,
        out_specs=(vmem, vmem, hbm, hbm, hbm, hbm),
        scratch_shapes=[
            row_buffer,
            row_buffer,
            pltpu.VMEM((rows, 2 * ff), F32),
            pltpu.VMEM((rows, ff), BF16),
            pltpu.VMEM((width, 2 * ff), BF16),
            pltpu.VMEM((ff, width), BF16),
            pltpu.VMEM((rows, 2 * ff), BF16),
            row_buffer,
            pltpu.VMEM((2, PLANE, ROWS, width), BF16),
            pltpu.VMEM((rows, 512), BF16),
            pltpu.VMEM((rows, 512), BF16),
            pltpu.VMEM((rows, 512), BF16),
            pltpu.VMEM((512, TILE), F32),
            pltpu.VMEM((2, 512, width), BF16),
            pltpu.VMEM((2, 128, width), F32),
            pltpu.VMEM((2, 3, 128, width), BF16),
            pltpu.VMEM((WIDE, 2 * ff), F32),
            *slabs,
            *slabs,
            dma((7,)), dma((chunks,)), dma((chunks,)), dma((chunks,)), dma((chunks,)), dma((chunks,)),
            dma((2,)), dma((2, 15)), dma((2, 15)), dma((2, 3)), dma((2, 3)),
        ],
        compiler_params=pltpu.CompilerParams(
            collective_id=1, has_side_effects=True, vmem_limit_bytes=63 * 2**20
        ),
    )(x, og, eo, pre, hid, meta, wg, wu, wd)


def body(tokens, cotangent, expert_ids, combine, placement, moves, w_gate, w_up, w_down):
    weights = (w_gate[0], w_up[0], w_down[0])
    ff = weights[0].shape[1]
    mine = jnp.arange(moves.shape[0]) == lax.axis_index("expert")
    moved = jnp.sum(jnp.where(mine, moves, 0)) > 0
    x, og, meta, pre, hid, eo = dispatch(
        expert_ids.T, combine.T, placement[:, None], tokens, cotangent, *weights
    )
    mixed, input_grad, own_down, own_wide, got_down, got_wide = finish(
        x, og, eo, pre, hid, meta, *weights
    )
    down = jnp.where(moved, got_down, own_down).astype(F32)
    gate = jnp.where(moved, got_wide[:, :ff], own_wide[:, :ff]).astype(F32)
    up = jnp.where(moved, got_wide[:, ff:], own_wide[:, ff:]).astype(F32)
    return mixed, input_grad, gate[None], up[None], down[None]


def solution(mesh):
    tok = P(("dp", "expert"), None)
    weight = P("expert", None, None)
    grad = P("expert", "dp", None)
    return jax.shard_map(
        body,
        mesh=mesh,
        in_specs=(tok, tok, tok, tok, P(), P(), weight, weight, weight),
        out_specs=(tok, tok, grad, grad, grad),
        check_vma=False,
    )
```

time: 336 us -> 284 us (0.85)
  matrix products: 44.8 us -> 0 us
    dot_general x12 -> x0, matrix products: 44.8 us -> none  [the longest x3 11.9 us: halves(): lax.dot_general(mine, right, CONTRACT_ROWS, preferred_element_type=F32)]
    pallas_call x1, Pallas kernels: 177 us -> 173 us  [finish(): pl.pallas_call(finish_kernel, name='finish', out_shape=(row_shape, row_sh...]
where the time goes in v2:
time: 284 us; the launch traced here: 282 us
  Pallas kernels  270 us (95%)
  other arithmetic  7.18 us (3%)
  local copies, waits for them, and re-layouts  3.96 us (1%)
    pallas_call x1, Pallas kernels, finish(): pl.pallas_call(finish_kernel, name='finish', out_shape=(row_shape, row_sh...  173 us
    pallas_call x1, Pallas kernels, dispatch(): pl.pallas_call(dispatch_kernel, name='dispatch', out_shape=(row_shape, ro...  97.1 us
    broadcast_in_dim x2, other arithmetic, body(): return (mixed, input_grad, gate[None], up[None], down[None])  6.55 us

profile of v2, /device:TPU:1, one launch (start us, length us, event | category | flops | bytes accessed | tf_op | source)
XLA Modules:
  0.0 282.4 jit_solution(8940732118375597513)
XLA Ops:
  0.6 1.4 copy.14.plc
  2.0 97.1 %dispatch.1 = (bf16[16,48,2048]{2,1,0:T(8,128)(2,1)}, bf16[16,48,2048]{2,1,0:T(8,128)(2,1)}, f32[4,8,128]{2,1,0:T(8,128)}, f32[768,1536]{1,0:T(8,128)}, bf16[768...) custom-call(s32[4,128]{1,0:T(4,128)} %bitcast.21, f32[4,128]{1,0:T(4,128)} %bitcast.22, s32[64,1]{1,0:T(8,128)} %copy.14.plc, ...), custom_call_target="tpu_custom_call" | custom-call | tf_op jit(solution)/shard_map/dispatch/pallas_call | solution.py:212
  99.1 0.0 copy-start.4
  99.1 172.8 %finish.1 = (bf16[128,2048]{1,0:T(8,128)(2,1)}, bf16[128,2048]{1,0:T(8,128)(2,1)}, bf16[384,2048]{1,0:T(8,128)(2,1)}, bf16[1024,1536]{1,0:T(8,128)(2,1)}, bf16[3...) custom-call(bf16[16,48,2048]{2,1,0:T(8,128)(2,1)} %get-tuple-element.17.x_in, ...), custom_call_target="tpu_custom_call" | custom-call | tf_op jit(solution)/shard_map/finish/pallas_call | solution.py:459
  271.9 0.0 copy-done.4
  271.9 0.6 fusion
  273.2 0.0 copy-start
  273.2 0.0 copy-start.1
  273.2 3.4 %bitcast_convert_fusion = f32[1,384,2048]{2,1,0:T(8,128)} fusion(bf16[384,2048]{1,0:T(8,128)(2,1)} %get-tuple-element.27, bf16[384,2048]{1,0:T(8,128)(2,1)} %get-tuple-element.28, pred[]{:T(512)S(6)} %gt.3), kind=kLoop, calls=%fused_computation | loop fusion | flops 1572864 | bytes 6291457 | tf_op jit(solution)/shard_map/broadcast_in_dim | solution.py:508
  276.7 0.0 copy-done
  276.7 1.0 copy-done.1
  277.7 0.0 copy-start.3
  277.7 0.0 copy-start.2
  277.7 3.1 %bitcast_convert_fusion.1 = (f32[1,1024,768]{2,1,0:T(8,128)}, f32[1,1024,768]{2,1,0:T(8,128)}) fusion(bf16[1024,1536]{1,0:T(8,128)(2,1)S(1)} %copy-done, bf16[1024,1536]{1,0:T(8,128)(2,1)S(1)} %copy-done.1, pred[]{:T(512)S(6)} %gt.3), kind=kLoop, calls=%fused_computation.1 | loop fusion | flops 3145728 | bytes 12582913 | tf_op jit(solution)/shard_map/broadcast_in_dim | solution.py:508
  280.8 0.0 copy-done.3
  280.8 0.8 copy.17
  281.6 0.0 copy-done.2
  281.6 0.8 copy.18
Async XLA Ops:
  99.1 172.8 %copy-start.4 = (s32[64]{0:T(128)S(1)}, s32[64]{0:T(128)}, u32[]{:S(2)}) copy-start(s32[64]{0:T(128)} %param.14) | copy-start | bytes 772
  273.2 3.5 %copy-start = (bf16[1024,1536]{1,0:T(8,128)(2,1)S(1)}, bf16[1024,1536]{1,0:T(8,128)(2,1)}, u32[]{:S(2)}) copy-start(bf16[1024,1536]{1,0:T(8,128)(2,1)} %get-tuple-element.26) | copy-start | bytes 9437188
  273.2 4.4 %copy-start.1 = (bf16[1024,1536]{1,0:T(8,128)(2,1)S(1)}, bf16[1024,1536]{1,0:T(8,128)(2,1)}, u32[]{:S(2)}) copy-start(bf16[1024,1536]{1,0:T(8,128)(2,1)} %get-tuple-element.25) | copy-start | bytes 9437188
  277.7 3.1 %copy-start.3 = (bf16[128,2048]{1,0:T(8,128)(2,1)S(1)}, bf16[128,2048]{1,0:T(8,128)(2,1)}, u32[]{:S(2)}) copy-start(bf16[128,2048]{1,0:T(8,128)(2,1)} %get-tuple-element.36) | copy-start | bytes 1572868
  277.7 3.9 %copy-start.2 = (bf16[128,2048]{1,0:T(8,128)(2,1)S(1)}, bf16[128,2048]{1,0:T(8,128)(2,1)}, u32[]{:S(2)}) copy-start(bf16[128,2048]{1,0:T(8,128)(2,1)} %get-tuple-element.37) | copy-start | bytes 1572868

commit v3 on v2

--- a/solution.py
+++ b/solution.py
@@ -70,6 +70,12 @@
     return hit, weight
 
 
+def moving(table, p, l, y):
+    slot = lax.broadcasted_iota(jnp.int32, (table.shape[0], 1), 0)
+    mine = jnp.where(slot == y * PLANE + l, table[:, 1:2], 0)
+    return jnp.sum(mine.astype(F32), axis=0, keepdims=True) > 0.0
+
+
 def load(src, dst, sem):
     copy = pltpu.make_async_copy(src, dst, sem)
     copy.start()
@@ -77,9 +83,11 @@
 
 
 def dispatch_kernel(
-    ids, comb, plc, tok, cot, wg, wu, wd, x_out, og_out, meta, pre_out, hid_out, eo_out,
-    gtok, gcot, pick, rw, sx, so, x, wgu, wdv, pre, hid, eo,
+    ids, comb, table, tok, cot, wg, wu, wd,
+    x_out, og_out, meta, pre_out, hid_out, eo_out, wgu_out, wd_out,
+    gtok, gcot, pick, rw, sx, so, x, wgu, wdv, pre, hid, eo, new_wide, new_down,
     meta_send, meta_recv, ag_send, ag_recv, own_sem, d_send, d_recv, w_sem, out_sem,
+    swap_send, swap_recv, pass_send, pass_recv,
 ):
     p, l, y = place()
     width = tok.shape[1]
@@ -87,17 +95,57 @@
     half = width // 2
     ring = [ring_peer(p, l, y, d) for d in range(1, RINGS)]
     peers = [plane_peer(p, l, y, r) for r in range(1, PLANE)]
-    ready = greet(ring + [d for d, _ in peers])
-    weights = [
-        load(wg, wgu.at[:, pl.ds(0, ff)], w_sem.at[0]),
-        load(wu, wgu.at[:, pl.ds(ff, ff)], w_sem.at[1]),
-        load(wd, wdv, w_sem.at[2]),
+    across = (1 - p, y * PLANE + l)
+    ready = greet(ring + [d for d, _ in peers] + [across])
+    odd = lax.rem(l, 2) == 1
+    wide_half, down_half = width // 2, ff // 2
+    wide_rows = pl.ds(pl.multiple_of(p * wide_half, wide_half), wide_half)
+    down_rows = pl.ds(pl.multiple_of(p * down_half, down_half), down_half)
+    whole = [
+        pltpu.make_async_copy(wg, wgu.at[:, pl.ds(0, ff)], w_sem.at[0]),
+        pltpu.make_async_copy(wu, wgu.at[:, pl.ds(ff, ff)], w_sem.at[1]),
+        pltpu.make_async_copy(wd, wdv, w_sem.at[2]),
     ]
-
-    slots = plc.shape[0]
+    partly = [
+        pltpu.make_async_copy(wg.at[wide_rows], wgu.at[wide_rows, pl.ds(0, ff)], w_sem.at[0]),
+        pltpu.make_async_copy(wu.at[wide_rows], wgu.at[wide_rows, pl.ds(ff, ff)], w_sem.at[1]),
+        pltpu.make_async_copy(wd.at[down_rows], wdv.at[down_rows], w_sem.at[2]),
+    ]
+    swaps, passes, pieces = [], [], []
+    for i in range(6):
+        which = i // 2
+        size = (wide_half if which < 2 else down_half) // 2
+        source = (wg, wu, wd)[which]
+        at = pl.ds(pl.multiple_of(p * 2 * size + (i % 2) * size, size), size)
+        near = pl.ds((i % 2) * size, size)
+        if which < 2:
+            landed = new_wide.at[near, pl.ds(which * ff, ff)]
+            held = wgu.at[at, pl.ds(which * ff, ff)]
+        else:
+            landed = new_down.at[near]
+            held = wdv.at[at]
+        swaps.append(remote(source.at[at], landed, swap_send.at[i], swap_recv.at[i], ring[1]))
+        passes.append(remote(held, held, pass_send.at[i], pass_recv.at[i], across))
+        pieces.append((landed, held, size))
+
+    @pl.when(odd)
+    def _():
+        for copy in partly:
+            copy.start()
+
+    @pl.when(jnp.logical_not(odd))
+    def _():
+        for copy in whole:
+            copy.start()
+
+    slots = table.shape[0]
     tokens = ids.shape[1]
     slot_id = lax.broadcasted_iota(jnp.int32, (slots, tokens), 0)
-    owned = [(plc[...] == ids[k : k + 1, :]) for k in range(4)]
+    plc, moves = table[:, 0:1], table[:, 1:2]
+    paired = jnp.concatenate([plc[slots // 2 :], plc[: slots // 2]], axis=0)
+    one = lax.broadcasted_iota(jnp.int32, (slots, 1), 0)
+    located = jnp.where((lax.rem(one, 2) == 1) & (moves == 1), paired, plc)
+    owned = [(located == ids[k : k + 1, :]) for k in range(4)]
     member = jnp.zeros((slots, tokens), F32)
     for o in owned:
         member = jnp.where(o, 1.0, member)
@@ -141,6 +189,12 @@
         cols = pl.ds((c % 2) * half, half)
         for copy in gather[c]:
             copy.wait_recv()
+        if c == 2:
+
+            @pl.when(odd)
+            def _():
+                for copy in swaps:
+                    copy.start()
 
         def step(n, _, src=src, buf=buf, c=c):
             at = columns((c % 2) * (half // TILE) + n)
@@ -164,8 +218,25 @@
         for copy in sent[c]:
             copy.wait_recv()
     outs = [load(x, x_out, out_sem.at[0])]
-    for copy in weights:
-        copy.wait()
+
+    @pl.when(jnp.logical_not(odd))
+    def _():
+        for copy in whole:
+            copy.wait()
+
+    @pl.when(odd)
+    def _():
+        for copy in partly:
+            copy.wait()
+        take = moving(table, p, l, y)
+        for i, (landed, held, size) in enumerate(pieces):
+            swaps[i].wait_recv()
+            held[...] = jnp.where(take, landed[...].astype(F32), held[...].astype(F32)).astype(BF16)
+            passes[i].start()
+        for copy in passes[:4]:
+            copy.wait_recv()
+
+    outs.append(load(wgu, wgu_out, out_sem.at[4]))
 
     def forward(n, _):
         gate_at = columns(n)
@@ -182,6 +253,13 @@
     outs.append(load(pre, pre_out, out_sem.at[1]))
     outs.append(load(hid, hid_out, out_sem.at[2]))
 
+    @pl.when(odd)
+    def _():
+        for copy in passes[4:]:
+            copy.wait_recv()
+
+    outs.append(load(wdv, wd_out, out_sem.at[5]))
+
     def project(n, _):
         at = columns(n)
         got = jnp.dot(hid[...], wdv[:, at], preferred_element_type=F32)
@@ -199,8 +277,13 @@
     for copy in copies + [g for group in gather + sent for g in group]:
         copy.wait_send()
 
-
-def dispatch(ids, comb, plc, tok, cot, wg, wu, wd):
+    @pl.when(odd)
+    def _():
+        for copy in swaps + passes:
+            copy.wait_send()
+
+
+def dispatch(ids, comb, table, tok, cot, wg, wu, wd):
     width = tok.shape[1]
     ff = wg.shape[1]
     rows = PLANE * ROWS
@@ -219,9 +302,11 @@
             jax.ShapeDtypeStruct((rows, 2 * ff), F32),
             jax.ShapeDtypeStruct((rows, ff), BF16),
             row_shape,
+            jax.ShapeDtypeStruct((width, 2 * ff), BF16),
+            jax.ShapeDtypeStruct((ff, width), BF16),
         ),
         in_specs=[vmem] * 5 + [hbm] * 3,
-        out_specs=(hbm, hbm, vmem, hbm, hbm, hbm),
+        out_specs=(hbm, hbm, vmem, hbm, hbm, hbm, hbm, hbm),
         scratch_shapes=[
             pltpu.VMEM((512, width), BF16),
             pltpu.VMEM((512, width), BF16),
@@ -235,13 +320,15 @@
             pltpu.VMEM((rows, 2 * ff), F32),
             pltpu.VMEM((rows, ff), BF16),
             row_buffer,
+            pltpu.VMEM((width // 2, 2 * ff), BF16),
+            pltpu.VMEM((ff // 2, width), BF16),
             dma((3,)), dma((3,)), dma((4, 3)), dma((4, 3)), dma((4,)), dma((4, 15)), dma((4, 15)),
-            dma((3,)), dma((4,)),
+            dma((3,)), dma((6,)), dma((6,)), dma((6,)), dma((6,)), dma((6,)),
         ],
         compiler_params=pltpu.CompilerParams(
             collective_id=0, has_side_effects=True, vmem_limit_bytes=60 * 2**20
         ),
-    )(ids, comb, plc, tok, cot, wg, wu, wd)
+    )(ids, comb, table, tok, cot, wg, wu, wd)
 
 
 DOWN = 128
@@ -250,10 +337,10 @@
 
 
 def finish_kernel(
-    x_in, og_in, eo, pre_in, hid_in, meta, wg, wu, wd,
-    mixed, input_grad, own_down, own_wide, got_down, got_wide,
-    x, og, pre, hid, wgu, wdv, gu, rg, ret, whi, wlo, pick, acc, part, own, gath, fresh,
-    oth_down, oth_wide, x_down, x_wide,
+    x_in, og_in, eo, pre_in, hid_in, meta, table, wgu_in, wd_in,
+    mixed, input_grad, own_down, own_wide,
+    x, og, pre, hid, wgu, wdv, gu, rg, ret, whi, wlo, pick, acc, part, own, gath,
+    oth_down, oth_wide, x_down, x_wide, got_down, got_wide,
     in_sem, x_send, x_recv, y_send, y_recv, s_sem, own_sem, p_send, p_recv, b_send, b_recv,
 ):
     p, l, y = place()
@@ -267,12 +354,13 @@
     loads = [
         load(hid_in, hid, in_sem.at[0]),
         load(og_in, og, in_sem.at[1]),
-        load(wd, wdv, in_sem.at[2]),
+        load(wd_in, wdv, in_sem.at[2]),
         load(pre_in, pre, in_sem.at[3]),
         load(x_in, x, in_sem.at[4]),
-        load(wg, wgu.at[:, pl.ds(0, ff)], in_sem.at[5]),
-        load(wu, wgu.at[:, pl.ds(ff, ff)], in_sem.at[6]),
+        load(wgu_in, wgu, in_sem.at[5]),
     ]
+    even = lax.rem(l, 2) == 0
+    fresh = pre
     downs = (ff // 2) // DOWN
     narrows = (width // 2) // NARROW
     chunks = downs + narrows
@@ -322,7 +410,7 @@
         for n in range(width // 512):
             cols = slice(n * 512, (n + 1) * 512)
             oth_down[c * DOWN : (c + 1) * DOWN, cols] = (0.5 * part_of(cols)).astype(BF16)
-        x_copies[c].start()
+        pl.when(even)(x_copies[c].start)
         if c == 0:
             for copy in back[0]:
                 copy.start()
@@ -350,9 +438,8 @@
             cols = slice(n * ff, (n + 1) * ff)
             oth_wide[c * WIDE : (c + 1) * WIDE, cols] = (0.5 * part_of(cols)).astype(BF16)
         for i in range(per):
-            x_copies[downs + c * per + i].start()
+            pl.when(even)(x_copies[downs + c * per + i].start)
     loads[5].wait()
-    loads[6].wait()
 
     def pull(n, _):
         at = columns(n)
@@ -401,7 +488,7 @@
             copy.start()
             summed[which].append(copy)
 
-    for c in range(chunks):
+    def reduce(c):
         if c < downs:
             part_of = down_part(p, c)
             at = slice(c * DOWN, (c + 1) * DOWN)
@@ -415,35 +502,64 @@
                 part_of = wide_part(p, i // per)
                 for n in range(2):
                     cols = slice(n * ff, (n + 1) * ff)
-                    fresh[:, cols] = 0.5 * part_of(cols)
+                    fresh[0:WIDE, cols] = 0.5 * part_of(cols)
             at = slice(i * NARROW, (i + 1) * NARROW)
             x_copies[c].wait_recv()
             mine = fresh[(i % per) * NARROW : (i % per + 1) * NARROW, :]
             x_wide[at, :] = (mine + x_wide[at, :].astype(F32)).astype(BF16)
-        y_copies[c].start()
-        kept[c].start()
-        if c == EARLY:
-            combine(0)
-        if c == LATE:
-            combine(1)
+
+    @pl.when(even)
+    def _():
+        for c in range(EARLY):
+            reduce(c)
+            y_copies[c].start()
+
+    combine(0)
+
+    @pl.when(even)
+    def _():
+        for c in range(EARLY, chunks):
+            reduce(c)
+            y_copies[c].start()
+
+    @pl.when(jnp.logical_not(even))
+    def _():
+        for copy in x_copies:
+            copy.start()
+
+    combine(1)
+
+    @pl.when(even)
+    def _():
+        take = moving(table, p, l, y)
+        for c in range(chunks):
+            y_copies[c].wait()
+            mine, got = slab(c, x_down, x_wide), slab(c, got_down, got_wide)
+            mine[...] = jnp.where(take, got[...].astype(F32), mine[...].astype(F32)).astype(BF16)
+            kept[c].start()
+
+    @pl.when(jnp.logical_not(even))
+    def _():
+        for c in range(chunks):
+            reduce(c)
+            kept[c].start()
+
     for which, out in enumerate((mixed, input_grad)):
         total = own[which]
         for d in range(3):
             summed[which][d].wait_recv()
             total += gath[which, d].astype(F32)
         out[...] = total.astype(BF16)
-    for c in range(chunks):
-        y_copies[c].wait()
-        kept[c].wait()
+    for copy in kept:
+        copy.wait()
     for copy in back[0][:-1] + back[1][:-1] + x_copies + summed[0] + summed[1]:
         copy.wait_send()
 
 
-EARLY = 2
-LATE = 7
-
-
-def finish(x, og, eo, pre, hid, meta, wg, wu, wd):
+EARLY = 8
+
+
+def finish(x, og, eo, pre, hid, meta, table, wgu, wd):
     width = x.shape[-1]
     ff = hid.shape[1]
     rows = PLANE * ROWS
@@ -459,9 +575,9 @@
     return pl.pallas_call(
         finish_kernel,
         name="finish",
-        out_shape=(row_shape, row_shape, *grads, *grads),
-        in_specs=[hbm] * 5 + [vmem] + [hbm] * 3,
-        out_specs=(vmem, vmem, hbm, hbm, hbm, hbm),
+        out_shape=(row_shape, row_shape, *grads),
+        in_specs=[hbm] * 5 + [vmem] * 2 + [hbm] * 2,
+        out_specs=(vmem, vmem, hbm, hbm),
         scratch_shapes=[
             row_buffer,
             row_buffer,
@@ -479,33 +595,28 @@
             pltpu.VMEM((2, 512, width), BF16),
             pltpu.VMEM((2, 128, width), F32),
             pltpu.VMEM((2, 3, 128, width), BF16),
-            pltpu.VMEM((WIDE, 2 * ff), F32),
             *slabs,
             *slabs,
-            dma((7,)), dma((chunks,)), dma((chunks,)), dma((chunks,)), dma((chunks,)), dma((chunks,)),
+            *slabs,
+            dma((6,)), dma((chunks,)), dma((chunks,)), dma((chunks,)), dma((chunks,)), dma((chunks,)),
             dma((2,)), dma((2, 15)), dma((2, 15)), dma((2, 3)), dma((2, 3)),
         ],
         compiler_params=pltpu.CompilerParams(
             collective_id=1, has_side_effects=True, vmem_limit_bytes=63 * 2**20
         ),
-    )(x, og, eo, pre, hid, meta, wg, wu, wd)
+    )(x, og, eo, pre, hid, meta, table, wgu, wd)
 
 
 def body(tokens, cotangent, expert_ids, combine, placement, moves, w_gate, w_up, w_down):
     weights = (w_gate[0], w_up[0], w_down[0])
     ff = weights[0].shape[1]
-    mine = jnp.arange(moves.shape[0]) == lax.axis_index("expert")
-    moved = jnp.sum(jnp.where(mine, moves, 0)) > 0
-    x, og, meta, pre, hid, eo = dispatch(
-        expert_ids.T, combine.T, placement[:, None], tokens, cotangent, *weights
+    table = jnp.stack([placement, moves], axis=1)
+    x, og, meta, pre, hid, eo, wgu, wd = dispatch(
+        expert_ids.T, combine.T, table, tokens, cotangent, *weights
     )
-    mixed, input_grad, own_down, own_wide, got_down, got_wide = finish(
-        x, og, eo, pre, hid, meta, *weights
-    )
-    down = jnp.where(moved, got_down, own_down).astype(F32)
-    gate = jnp.where(moved, got_wide[:, :ff], own_wide[:, :ff]).astype(F32)
-    up = jnp.where(moved, got_wide[:, ff:], own_wide[:, ff:]).astype(F32)
-    return mixed, input_grad, gate[None], up[None], down[None]
+    mixed, input_grad, down, wide = finish(x, og, eo, pre, hid, meta, table, wgu, wd)
+    gate, up = wide[:, :ff], wide[:, ff:]
+    return (mixed, input_grad) + tuple(g.astype(F32)[None] for g in (gate, up, down))
 
 
 def solution(mesh):

time: 284 us -> 259 us (0.912)
  Pallas kernels: 270 us -> 249 us
    pallas_call x1, Pallas kernels: 173 us -> 122 us  [finish(): pl.pallas_call(finish_kernel, name='finish', out_shape=(row_shape, row_sh...]
    pallas_call x1, Pallas kernels: 97.1 us -> 126 us  [dispatch(): pl.pallas_call(dispatch_kernel, name='dispatch', out_shape=(row_shape, ro...]
where the time goes in v3:
time: 259 us
  Pallas kernels  249 us (96%)
  other arithmetic  7.41 us (3%)
    pallas_call x1, Pallas kernels, dispatch(): pl.pallas_call(dispatch_kernel, name='dispatch', out_shape=(row_shape, ro...  126 us
    pallas_call x1, Pallas kernels, finish(): pl.pallas_call(finish_kernel, name='finish', out_shape=(row_shape, row_sh...  122 us
    broadcast_in_dim x2, other arithmetic, body(): g.astype(F32)[None]  6.73 us

profile of v3, /device:TPU:1, one launch (start us, length us, event | category | flops | bytes accessed | tf_op | source)
XLA Modules:
  0.0 258.9 jit_solution(6124356866519487601)
XLA Ops:
  0.6 0.7 pad_add_fusion
  1.3 0.7 copy.16.table
  2.0 126.1 %dispatch.1 = (bf16[16,48,2048]{2,1,0:T(8,128)(2,1)}, bf16[16,48,2048]{2,1,0:T(8,128)(2,1)}, f32[4,8,128]{2,1,0:T(8,128)}, f32[768,1536]{1,0:T(8,128)}, bf16[768...) custom-call(s32[4,128]{1,0:T(4,128)} %bitcast.19, ...), custom_call_target="tpu_custom_call" | custom-call | tf_op jit(solution)/shard_map/dispatch/pallas_call | solution.py:295
  128.2 122.4 %finish.1 = (bf16[128,2048]{1,0:T(8,128)(2,1)}, bf16[128,2048]{1,0:T(8,128)(2,1)}, bf16[384,2048]{1,0:T(8,128)(2,1)}, bf16[1024,1536]{1,0:T(8,128)(2,1)}) custom-call(bf16[16,48,2048]{2,1,0:T(8,128)(2,1)} %get-tuple-element.17.x_in, bf16[16,48,2048]{2,1,0:T(8,128)(2,1)} %get-tuple-element.18.og_in, bf16[16,48,2048]{2,1,0:T(8,128)(2,1)} %get-tuple-element.19.eo, ...), custom_call_target="tpu_custom_call" | custom-call | tf_op jit(solution)/shard_map/finish/pallas_call | solution.py:575
  250.6 0.0 copy-start
  250.6 3.6 %bitcast_convert_fusion = f32[1,384,2048]{2,1,0:T(8,128)} fusion(bf16[384,2048]{1,0:T(8,128)(2,1)} %get-tuple-element.28), kind=kLoop, calls=%fused_computation | loop fusion | flops 786432 | bytes 4718592 | tf_op jit(solution)/shard_map/broadcast_in_dim | solution.py:619
  254.2 0.0 copy-done
  254.2 0.0 copy-start.2
  254.2 0.0 copy-start.1
  254.2 3.1 %bitcast_convert_fusion.1 = (f32[1,1024,768]{2,1,0:T(8,128)}, f32[1,1024,768]{2,1,0:T(8,128)}) fusion(bf16[1024,1536]{1,0:T(8,128)(2,1)S(1)} %copy-done), kind=kLoop, calls=%fused_computation.1 | loop fusion | flops 1572864 | bytes 9437184 | tf_op jit(solution)/shard_map/broadcast_in_dim | solution.py:619
  257.3 0.0 copy-done.2
  257.3 0.8 copy.20
  258.1 0.0 copy-done.1
  258.1 0.8 copy.21
Async XLA Ops:
  250.6 3.6 %copy-start = (bf16[1024,1536]{1,0:T(8,128)(2,1)S(1)}, bf16[1024,1536]{1,0:T(8,128)(2,1)}, u32[]{:S(2)}) copy-start(bf16[1024,1536]{1,0:T(8,128)(2,1)} %get-tuple-element.27) | copy-start | bytes 9437188
  254.2 3.1 %copy-start.2 = (bf16[128,2048]{1,0:T(8,128)(2,1)S(1)}, bf16[128,2048]{1,0:T(8,128)(2,1)}, u32[]{:S(2)}) copy-start(bf16[128,2048]{1,0:T(8,128)(2,1)} %get-tuple-element.36) | copy-start | bytes 1572868
  254.2 3.9 %copy-start.1 = (bf16[128,2048]{1,0:T(8,128)(2,1)S(1)}, bf16[128,2048]{1,0:T(8,128)(2,1)}, u32[]{:S(2)}) copy-start(bf16[128,2048]{1,0:T(8,128)(2,1)} %get-tuple-element.37) | copy-start | bytes 1572868

commit v4 on v3

--- a/solution.py
+++ b/solution.py
@@ -82,10 +82,13 @@
     return copy
 
 
+PIECES = 4
+
+
 def dispatch_kernel(
     ids, comb, table, tok, cot, wg, wu, wd,
-    x_out, og_out, meta, pre_out, hid_out, eo_out, wgu_out, wd_out,
-    gtok, gcot, pick, rw, sx, so, x, wgu, wdv, pre, hid, eo, new_wide, new_down,
+    x_out, og_out, meta, pre_out, hid_out, wgu_out, wd_out, eo_out,
+    gtok, gcot, pick, rw, sx, so, x, wgu, wdv, pre, hid, new_wide, new_down, eo,
     meta_send, meta_recv, ag_send, ag_recv, own_sem, d_send, d_recv, w_sem, out_sem,
     swap_send, swap_recv, pass_send, pass_recv,
 ):
@@ -112,12 +115,12 @@
         pltpu.make_async_copy(wd.at[down_rows], wdv.at[down_rows], w_sem.at[2]),
     ]
     swaps, passes, pieces = [], [], []
-    for i in range(6):
-        which = i // 2
-        size = (wide_half if which < 2 else down_half) // 2
+    for i in range(3 * PIECES):
+        which, piece = i // PIECES, i % PIECES
+        size = (wide_half if which < 2 else down_half) // PIECES
         source = (wg, wu, wd)[which]
-        at = pl.ds(pl.multiple_of(p * 2 * size + (i % 2) * size, size), size)
-        near = pl.ds((i % 2) * size, size)
+        at = pl.ds(pl.multiple_of(p * PIECES * size + piece * size, size), size)
+        near = pl.ds(piece * size, size)
         if which < 2:
             landed = new_wide.at[near, pl.ds(which * ff, ff)]
             held = wgu.at[at, pl.ds(which * ff, ff)]
@@ -126,7 +129,15 @@
             held = wdv.at[at]
         swaps.append(remote(source.at[at], landed, swap_send.at[i], swap_recv.at[i], ring[1]))
         passes.append(remote(held, held, pass_send.at[i], pass_recv.at[i], across))
-        pieces.append((landed, held, size))
+        pieces.append((landed, held))
+
+    take = moving(table, p, l, y)
+
+    def settle(i):
+        landed, held = pieces[i]
+        swaps[i].wait_recv()
+        held[...] = jnp.where(take, landed[...].astype(F32), held[...].astype(F32)).astype(BF16)
+        passes[i].start()
 
     @pl.when(odd)
     def _():
@@ -189,7 +200,7 @@
         cols = pl.ds((c % 2) * half, half)
         for copy in gather[c]:
             copy.wait_recv()
-        if c == 2:
+        if c == 1:
 
             @pl.when(odd)
             def _():
@@ -211,6 +222,16 @@
             copy.start()
             group.append(copy)
         sent.append(group)
+        if c >= 2:
+
+            @pl.when(odd)
+            def _(c=c):
+                if c == 2:
+                    for copy in partly:
+                        copy.wait()
+                for i in range(2 * (c - 2), 2 * (c - 1)):
+                    settle(i)
+
         own.append(load(buf.at[l, :, cols], dst.at[l, :, cols], own_sem.at[c]))
 
     for c in range(2):
@@ -226,54 +247,61 @@
 
     @pl.when(odd)
     def _():
-        for copy in partly:
-            copy.wait()
-        take = moving(table, p, l, y)
-        for i, (landed, held, size) in enumerate(pieces):
-            swaps[i].wait_recv()
-            held[...] = jnp.where(take, landed[...].astype(F32), held[...].astype(F32)).astype(BF16)
-            passes[i].start()
-        for copy in passes[:4]:
+        for i in range(4, 2 * PIECES):
+            settle(i)
+        for copy in passes[: 2 * PIECES]:
             copy.wait_recv()
 
-    outs.append(load(wgu, wgu_out, out_sem.at[4]))
-
-    def forward(n, _):
-        gate_at = columns(n)
-        up_at = columns(ff // TILE + n)
+    outs.append(load(wgu, wgu_out, out_sem.at[3]))
+    for n in range(ff // TILE):
+        gate_at = slice(n * TILE, (n + 1) * TILE)
+        up_at = slice(ff + n * TILE, ff + (n + 1) * TILE)
         rows = x[...].reshape(PLANE * ROWS, width)
         gate = jnp.dot(rows, wgu[:, gate_at], preferred_element_type=F32)
         up = jnp.dot(rows, wgu[:, up_at], preferred_element_type=F32)
         pre[:, gate_at] = gate
         pre[:, up_at] = up
         hid[:, gate_at] = (gate * jax.nn.sigmoid(gate) * up).astype(BF16)
-        return 0
-
-    lax.fori_loop(0, ff // TILE, forward, 0)
+
+        @pl.when(odd)
+        def _(n=n):
+            settle(2 * PIECES + n)
+
     outs.append(load(pre, pre_out, out_sem.at[1]))
     outs.append(load(hid, hid_out, out_sem.at[2]))
 
     @pl.when(odd)
     def _():
-        for copy in passes[4:]:
+        for i in range(2 * PIECES + ff // TILE, 3 * PIECES):
+            settle(i)
+        for copy in passes[2 * PIECES :]:
             copy.wait_recv()
 
-    outs.append(load(wdv, wd_out, out_sem.at[5]))
-
-    def project(n, _):
-        at = columns(n)
-        got = jnp.dot(hid[...], wdv[:, at], preferred_element_type=F32)
-        eo[:, :, at] = got.astype(BF16).reshape(PLANE, ROWS, TILE)
-        return 0
-
-    lax.fori_loop(0, width // TILE, project, 0)
-    outs.append(load(eo, eo_out, out_sem.at[3]))
+    outs.append(load(wdv, wd_out, out_sem.at[4]))
+    eo_copy = pltpu.make_async_copy(eo, eo_out, out_sem.at[0])
+
+    @pl.when(jnp.logical_not(odd))
+    def _():
+        def project(n, _):
+            at = columns(n)
+            eo[:, at] = jnp.dot(hid[...], wdv[:, at], preferred_element_type=F32).astype(BF16)
+            return 0
+
+        lax.fori_loop(0, width // TILE, project, 0)
+        outs[0].wait()
+        eo_copy.start()
+
+    @pl.when(odd)
+    def _():
+        outs[0].wait()
+
     for c in range(2, 4):
         own[c].wait()
         for copy in sent[c]:
             copy.wait_recv()
-    for copy in outs:
+    for copy in outs[1:]:
         copy.wait()
+    pl.when(jnp.logical_not(odd))(eo_copy.wait)
     for copy in copies + [g for group in gather + sent for g in group]:
         copy.wait_send()
 
@@ -301,9 +329,9 @@
             jax.ShapeDtypeStruct((RINGS, 8, 128), F32),
             jax.ShapeDtypeStruct((rows, 2 * ff), F32),
             jax.ShapeDtypeStruct((rows, ff), BF16),
-            row_shape,
             jax.ShapeDtypeStruct((width, 2 * ff), BF16),
             jax.ShapeDtypeStruct((ff, width), BF16),
+            jax.ShapeDtypeStruct((rows, width), BF16),
         ),
         in_specs=[vmem] * 5 + [hbm] * 3,
         out_specs=(hbm, hbm, vmem, hbm, hbm, hbm, hbm, hbm),
@@ -319,11 +347,11 @@
             pltpu.VMEM((ff, width), BF16),
             pltpu.VMEM((rows, 2 * ff), F32),
             pltpu.VMEM((rows, ff), BF16),
-            row_buffer,
             pltpu.VMEM((width // 2, 2 * ff), BF16),
             pltpu.VMEM((ff // 2, width), BF16),
+            pltpu.VMEM((rows, width), BF16),
             dma((3,)), dma((3,)), dma((4, 3)), dma((4, 3)), dma((4,)), dma((4, 15)), dma((4, 15)),
-            dma((3,)), dma((6,)), dma((6,)), dma((6,)), dma((6,)), dma((6,)),
+            dma((3,)), dma((5,)), *[dma((3 * PIECES,)) for _ in range(4)],
         ],
         compiler_params=pltpu.CompilerParams(
             collective_id=0, has_side_effects=True, vmem_limit_bytes=60 * 2**20
@@ -337,7 +365,7 @@
 
 
 def finish_kernel(
-    x_in, og_in, eo, pre_in, hid_in, meta, table, wgu_in, wd_in,
+    x_in, og_in, pre_in, hid_in, meta, table, wgu_in, wd_in, eo_in,
     mixed, input_grad, own_down, own_wide,
     x, og, pre, hid, wgu, wdv, gu, rg, ret, whi, wlo, pick, acc, part, own, gath,
     oth_down, oth_wide, x_down, x_wide, got_down, got_wide,
@@ -360,6 +388,8 @@
         load(wgu_in, wgu, in_sem.at[5]),
     ]
     even = lax.rem(l, 2) == 0
+    eo_copy = pltpu.make_async_copy(eo_in, part.at[pl.ds(0, rows_all)], in_sem.at[6])
+    pl.when(even)(eo_copy.start)
     fresh = pre
     downs = (ff // 2) // DOWN
     narrows = (width // 2) // NARROW
@@ -382,13 +412,21 @@
             x[:, :, at].reshape(rows_all, WIDE), gu[:, cols], CONTRACT_ROWS, preferred_element_type=F32
         )
 
+    def returned(which, j):
+        if which == 0:
+            return part.at[pl.ds(pl.multiple_of(j * ROWS, ROWS), ROWS)]
+        return rg.at[j]
+
     back = [[], []]
-    for which, source in enumerate((eo, rg)):
+    for which in range(2):
         for r, (device, j) in enumerate(peers):
+            source = returned(which, j)
             back[which].append(
-                remote(source.at[j], ret.at[which, l], p_send.at[which, r], p_recv.at[which, r], device)
+                remote(source, ret.at[which, l], p_send.at[which, r], p_recv.at[which, r], device)
             )
-        back[which].append(pltpu.make_async_copy(source.at[l], ret.at[which, l], own_sem.at[which]))
+        back[which].append(
+            pltpu.make_async_copy(returned(which, l), ret.at[which, l], own_sem.at[which])
+        )
     x_copies = [
         remote(slab(c, oth_down, oth_wide), slab(c, x_down, x_wide), x_send.at[c], x_recv.at[c], across)
         for c in range(chunks)
@@ -402,7 +440,20 @@
         for c in range(chunks)
     ]
 
+    def project(n, _):
+        at = columns(n)
+        got = jnp.dot(hid[...], wdv[:, at], preferred_element_type=F32)
+        part[0:rows_all, at] = got.astype(BF16)
+        return 0
+
     ready()
+
+    @pl.when(even)
+    def _():
+        eo_copy.wait()
+        for copy in back[0]:
+            copy.start()
+
     loads[0].wait()
     loads[1].wait()
     for c in range(downs):
@@ -412,9 +463,14 @@
             oth_down[c * DOWN : (c + 1) * DOWN, cols] = (0.5 * part_of(cols)).astype(BF16)
         pl.when(even)(x_copies[c].start)
         if c == 0:
-            for copy in back[0]:
-                copy.start()
-    loads[2].wait()
+            loads[2].wait()
+
+            @pl.when(jnp.logical_not(even))
+            def _():
+                lax.fori_loop(0, width // TILE, project, 0)
+                for copy in back[0]:
+                    copy.start()
+
     loads[3].wait()
 
     def backward(n, _):
@@ -465,6 +521,10 @@
         for copy in back[which][:-1]:
             copy.wait_recv()
         back[which][-1].wait()
+        if which == 0:
+            for copy in back[0][:-1]:
+                copy.wait_send()
+        blocks = which * RINGS * tokens
 
         def step(n, _):
             at = columns(n)
@@ -475,15 +535,15 @@
             else:
                 total = lax.dot_general(pick[...], rows, CONTRACT_ROWS, preferred_element_type=F32)
             acc[...] = total
-            part[which, :, at] = total.astype(BF16)
+            part[blocks : blocks + RINGS * tokens, at] = total.astype(BF16)
             own[which, :, at] = acc[own_rows, :]
             return 0
 
         lax.fori_loop(0, width // TILE, step, 0)
         for d in range(3):
-            there = pl.ds(pl.multiple_of(lax.rem(y + d + 1, RINGS) * tokens, tokens), tokens)
+            there = pl.ds(pl.multiple_of(blocks + lax.rem(y + d + 1, RINGS) * tokens, tokens), tokens)
             copy = remote(
-                part.at[which, there, :], gath.at[which, d], b_send.at[which, d], b_recv.at[which, d], ring[d]
+                part.at[there], gath.at[which, d], b_send.at[which, d], b_recv.at[which, d], ring[d]
             )
             copy.start()
             summed[which].append(copy)
@@ -552,14 +612,14 @@
         out[...] = total.astype(BF16)
     for copy in kept:
         copy.wait()
-    for copy in back[0][:-1] + back[1][:-1] + x_copies + summed[0] + summed[1]:
+    for copy in back[1][:-1] + x_copies + summed[0] + summed[1]:
         copy.wait_send()
 
 
 EARLY = 8
 
 
-def finish(x, og, eo, pre, hid, meta, table, wgu, wd):
+def finish(x, og, pre, hid, meta, table, wgu, wd, eo):
     width = x.shape[-1]
     ff = hid.shape[1]
     rows = PLANE * ROWS
@@ -576,7 +636,7 @@
         finish_kernel,
         name="finish",
         out_shape=(row_shape, row_shape, *grads),
-        in_specs=[hbm] * 5 + [vmem] * 2 + [hbm] * 2,
+        in_specs=[hbm] * 4 + [vmem] * 2 + [hbm] * 3,
         out_specs=(vmem, vmem, hbm, hbm),
         scratch_shapes=[
             row_buffer,
@@ -592,29 +652,29 @@
             pltpu.VMEM((rows, 512), BF16),
             pltpu.VMEM((rows, 512), BF16),
             pltpu.VMEM((512, TILE), F32),
-            pltpu.VMEM((2, 512, width), BF16),
+            pltpu.VMEM((2 * 512, width), BF16),
             pltpu.VMEM((2, 128, width), F32),
             pltpu.VMEM((2, 3, 128, width), BF16),
             *slabs,
             *slabs,
             *slabs,
-            dma((6,)), dma((chunks,)), dma((chunks,)), dma((chunks,)), dma((chunks,)), dma((chunks,)),
+            dma((7,)), dma((chunks,)), dma((chunks,)), dma((chunks,)), dma((chunks,)), dma((chunks,)),
             dma((2,)), dma((2, 15)), dma((2, 15)), dma((2, 3)), dma((2, 3)),
         ],
         compiler_params=pltpu.CompilerParams(
             collective_id=1, has_side_effects=True, vmem_limit_bytes=63 * 2**20
         ),
-    )(x, og, eo, pre, hid, meta, table, wgu, wd)
+    )(x, og, pre, hid, meta, table, wgu, wd, eo)
 
 
 def body(tokens, cotangent, expert_ids, combine, placement, moves, w_gate, w_up, w_down):
     weights = (w_gate[0], w_up[0], w_down[0])
     ff = weights[0].shape[1]
     table = jnp.stack([placement, moves], axis=1)
-    x, og, meta, pre, hid, eo, wgu, wd = dispatch(
+    x, og, meta, pre, hid, wgu, wd, eo = dispatch(
         expert_ids.T, combine.T, table, tokens, cotangent, *weights
     )
-    mixed, input_grad, down, wide = finish(x, og, eo, pre, hid, meta, table, wgu, wd)
+    mixed, input_grad, down, wide = finish(x, og, pre, hid, meta, table, wgu, wd, eo)
     gate, up = wide[:, :ff], wide[:, ff:]
     return (mixed, input_grad) + tuple(g.astype(F32)[None] for g in (gate, up, down))
 

time: 259 us -> 256 us (0.988)
  Pallas kernels: 249 us -> 245 us
    pallas_call x1, Pallas kernels: 126 us -> 123 us  [dispatch(): pl.pallas_call(dispatch_kernel, name='dispatch', out_shape=(row_shape, ro...]
where the time goes in v4:
time: 256 us; the launch traced here: 255 us
  Pallas kernels  245 us (96%)
  other arithmetic  7.41 us (3%)
    pallas_call x1, Pallas kernels, dispatch(): pl.pallas_call(dispatch_kernel, name='dispatch', out_shape=(row_shape, ro...  123 us
    pallas_call x1, Pallas kernels, finish(): pl.pallas_call(finish_kernel, name='finish', out_shape=(row_shape, row_sh...  122 us
    broadcast_in_dim x2, other arithmetic, body(): g.astype(F32)[None]  6.73 us

profile of v4, /device:TPU:1, one launch (start us, length us, event | category | flops | bytes accessed | tf_op | source)
XLA Modules:
  0.0 255.4 jit_solution(15331990481722989215)
XLA Ops:
  0.6 0.7 pad_add_fusion
  1.3 0.7 copy.16.table
  2.0 122.7 %dispatch.1 = (bf16[16,48,2048]{2,1,0:T(8,128)(2,1)}, bf16[16,48,2048]{2,1,0:T(8,128)(2,1)}, f32[4,8,128]{2,1,0:T(8,128)}, f32[768,1536]{1,0:T(8,128)}, bf16[768...) custom-call(s32[4,128]{1,0:T(4,128)} %bitcast.19, ...), custom_call_target="tpu_custom_call" | custom-call | tf_op jit(solution)/shard_map/dispatch/pallas_call | solution.py:323
  124.7 122.3 %finish.1 = (bf16[128,2048]{1,0:T(8,128)(2,1)}, bf16[128,2048]{1,0:T(8,128)(2,1)}, bf16[384,2048]{1,0:T(8,128)(2,1)}, bf16[1024,1536]{1,0:T(8,128)(2,1)}) custom-call(bf16[16,48,2048]{2,1,0:T(8,128)(2,1)} %get-tuple-element.17.x_in, bf16[16,48,2048]{2,1,0:T(8,128)(2,1)} %get-tuple-element.18.og_in, f32[768,1536]{1,0:T(8,128)} %get-tuple-element.19.pre_in, ...), custom_call_target="tpu_custom_call" | custom-call | tf_op jit(solution)/shard_map/finish/pallas_call | solution.py:635
  247.0 0.0 copy-start
  247.0 3.6 %bitcast_convert_fusion = f32[1,384,2048]{2,1,0:T(8,128)} fusion(bf16[384,2048]{1,0:T(8,128)(2,1)} %get-tuple-element.28), kind=kLoop, calls=%fused_computation | loop fusion | flops 786432 | bytes 4718592 | tf_op jit(solution)/shard_map/broadcast_in_dim | solution.py:679
  250.6 0.0 copy-done
  250.6 0.0 copy-start.2
  250.6 0.0 copy-start.1
  250.6 3.1 %bitcast_convert_fusion.1 = (f32[1,1024,768]{2,1,0:T(8,128)}, f32[1,1024,768]{2,1,0:T(8,128)}) fusion(bf16[1024,1536]{1,0:T(8,128)(2,1)S(1)} %copy-done), kind=kLoop, calls=%fused_computation.1 | loop fusion | flops 1572864 | bytes 9437184 | tf_op jit(solution)/shard_map/broadcast_in_dim | solution.py:679
  253.8 0.0 copy-done.2
  253.8 0.8 copy.20
  254.6 0.0 copy-done.1
  254.6 0.8 copy.21
Async XLA Ops:
  247.0 3.6 %copy-start = (bf16[1024,1536]{1,0:T(8,128)(2,1)S(1)}, bf16[1024,1536]{1,0:T(8,128)(2,1)}, u32[]{:S(2)}) copy-start(bf16[1024,1536]{1,0:T(8,128)(2,1)} %get-tuple-element.27) | copy-start | bytes 9437188
  250.6 3.1 %copy-start.2 = (bf16[128,2048]{1,0:T(8,128)(2,1)S(1)}, bf16[128,2048]{1,0:T(8,128)(2,1)}, u32[]{:S(2)}) copy-start(bf16[128,2048]{1,0:T(8,128)(2,1)} %get-tuple-element.36) | copy-start | bytes 1572868
  250.6 3.9 %copy-start.1 = (bf16[128,2048]{1,0:T(8,128)(2,1)S(1)}, bf16[128,2048]{1,0:T(8,128)(2,1)}, u32[]{:S(2)}) copy-start(bf16[128,2048]{1,0:T(8,128)(2,1)} %get-tuple-element.37) | copy-start | bytes 1572868

commit v5 on v4

--- a/solution.py
+++ b/solution.py
@@ -13,7 +13,6 @@
 CAP = 12
 ROWS = RINGS * CAP
 TILE = 256
-CONTRACT_ROWS = (((0,), (0,)), ((), ()))
 CONTRACT_LAST = (((1,), (1,)), ((), ()))
 
 
@@ -90,7 +89,7 @@
     x_out, og_out, meta, pre_out, hid_out, wgu_out, wd_out, eo_out,
     gtok, gcot, pick, rw, sx, so, x, wgu, wdv, pre, hid, new_wide, new_down, eo,
     meta_send, meta_recv, ag_send, ag_recv, own_sem, d_send, d_recv, w_sem, out_sem,
-    swap_send, swap_recv, pass_send, pass_recv,
+    swap_send, swap_recv, pass_send, pass_recv, keep_sem,
 ):
     p, l, y = place()
     width = tok.shape[1]
@@ -114,7 +113,7 @@
         pltpu.make_async_copy(wu.at[wide_rows], wgu.at[wide_rows, pl.ds(ff, ff)], w_sem.at[1]),
         pltpu.make_async_copy(wd.at[down_rows], wdv.at[down_rows], w_sem.at[2]),
     ]
-    swaps, passes, pieces = [], [], []
+    swaps, passes, pieces, keeps = [], [], [], []
     for i in range(3 * PIECES):
         which, piece = i // PIECES, i % PIECES
         size = (wide_half if which < 2 else down_half) // PIECES
@@ -128,7 +127,10 @@
             landed = new_down.at[near]
             held = wdv.at[at]
         swaps.append(remote(source.at[at], landed, swap_send.at[i], swap_recv.at[i], ring[1]))
-        passes.append(remote(held, held, pass_send.at[i], pass_recv.at[i], across))
+        final = held if which < 2 else wd_out.at[at]
+        passes.append(remote(held, final, pass_send.at[i], pass_recv.at[i], across))
+        if which == 2:
+            keeps.append(pltpu.make_async_copy(held, final, keep_sem.at[piece]))
         pieces.append((landed, held))
 
     take = moving(table, p, l, y)
@@ -138,6 +140,8 @@
         swaps[i].wait_recv()
         held[...] = jnp.where(take, landed[...].astype(F32), held[...].astype(F32)).astype(BF16)
         passes[i].start()
+        if i >= 2 * PIECES:
+            keeps[i - 2 * PIECES].start()
 
     @pl.when(odd)
     def _():
@@ -274,14 +278,13 @@
     def _():
         for i in range(2 * PIECES + ff // TILE, 3 * PIECES):
             settle(i)
-        for copy in passes[2 * PIECES :]:
-            copy.wait_recv()
-
-    outs.append(load(wdv, wd_out, out_sem.at[4]))
+    whole_down = pltpu.make_async_copy(wdv, wd_out, out_sem.at[4])
     eo_copy = pltpu.make_async_copy(eo, eo_out, out_sem.at[0])
 
     @pl.when(jnp.logical_not(odd))
     def _():
+        whole_down.start()
+
         def project(n, _):
             at = columns(n)
             eo[:, at] = jnp.dot(hid[...], wdv[:, at], preferred_element_type=F32).astype(BF16)
@@ -301,7 +304,19 @@
             copy.wait_recv()
     for copy in outs[1:]:
         copy.wait()
-    pl.when(jnp.logical_not(odd))(eo_copy.wait)
+
+    @pl.when(jnp.logical_not(odd))
+    def _():
+        eo_copy.wait()
+        whole_down.wait()
+
+    @pl.when(odd)
+    def _():
+        for copy in passes[2 * PIECES :]:
+            copy.wait_recv()
+        for copy in keeps:
+            copy.wait()
+
     for copy in copies + [g for group in gather + sent for g in group]:
         copy.wait_send()
 
@@ -351,7 +366,7 @@
             pltpu.VMEM((ff // 2, width), BF16),
             pltpu.VMEM((rows, width), BF16),
             dma((3,)), dma((3,)), dma((4, 3)), dma((4, 3)), dma((4,)), dma((4, 15)), dma((4, 15)),
-            dma((3,)), dma((5,)), *[dma((3 * PIECES,)) for _ in range(4)],
+            dma((3,)), dma((5,)), *[dma((3 * PIECES,)) for _ in range(4)], dma((PIECES,)),
         ],
         compiler_params=pltpu.CompilerParams(
             collective_id=0, has_side_effects=True, vmem_limit_bytes=60 * 2**20
@@ -402,30 +417,36 @@
 
     def down_part(side, c):
         at = pl.ds(pl.multiple_of(side * (ff // 2) + c * DOWN, DOWN), DOWN)
-        return lambda cols: lax.dot_general(
-            hid[:, at], og[:, :, cols].reshape(rows_all, -1), CONTRACT_ROWS, preferred_element_type=F32
+        left = hid[:, at].T
+        return lambda cols: jnp.dot(
+            left, og[:, :, cols].reshape(rows_all, -1), preferred_element_type=F32
         )
 
     def wide_part(side, c):
         at = pl.ds(pl.multiple_of(side * (width // 2) + c * WIDE, WIDE), WIDE)
-        return lambda cols: lax.dot_general(
-            x[:, :, at].reshape(rows_all, WIDE), gu[:, cols], CONTRACT_ROWS, preferred_element_type=F32
-        )
-
-    def returned(which, j):
-        if which == 0:
+        left = x[:, :, at].reshape(rows_all, WIDE).T
+        return lambda cols: jnp.dot(left, gu[:, cols], preferred_element_type=F32)
+
+    spans = [pl.ds(0, width), pl.ds(0, width // 2), pl.ds(width // 2, width // 2)]
+
+    def returned(group, j):
+        if group == 0:
             return part.at[pl.ds(pl.multiple_of(j * ROWS, ROWS), ROWS)]
-        return rg.at[j]
-
-    back = [[], []]
-    for which in range(2):
+        return rg.at[j, :, spans[group]]
+
+    def landing(group):
+        return ret.at[0, l] if group == 0 else ret.at[1, l, :, spans[group]]
+
+    back = [[], [], []]
+    for group in range(3):
         for r, (device, j) in enumerate(peers):
-            source = returned(which, j)
-            back[which].append(
-                remote(source, ret.at[which, l], p_send.at[which, r], p_recv.at[which, r], device)
+            back[group].append(
+                remote(
+                    returned(group, j), landing(group), p_send.at[group, r], p_recv.at[group, r], device
+                )
             )
-        back[which].append(
-            pltpu.make_async_copy(returned(which, l), ret.at[which, l], own_sem.at[which])
+        back[group].append(
+            pltpu.make_async_copy(returned(group, l), landing(group), own_sem.at[group])
         )
     x_copies = [
         remote(slab(c, oth_down, oth_wide), slab(c, x_down, x_wide), x_send.at[c], x_recv.at[c], across)
@@ -504,24 +525,26 @@
         return 0
 
     lax.fori_loop(0, width // TILE, pull, 0)
-    for copy in back[1]:
+    for copy in back[1] + back[2]:
         copy.start()
     for b in range(RINGS):
         hit, weight = selection(meta, y * PLANE * ROWS, b)
-        cols = slice(b * tokens, (b + 1) * tokens)
+        at = slice(b * tokens, (b + 1) * tokens)
+        weight = weight.T
         high = weight.astype(BF16)
-        pick[:, cols] = hit.astype(BF16)
-        whi[:, cols] = high
-        wlo[:, cols] = (weight - high.astype(F32)).astype(BF16)
+        pick[at, :] = hit.T.astype(BF16)
+        whi[at, :] = high
+        wlo[at, :] = (weight - high.astype(F32)).astype(BF16)
 
     own_rows = pl.ds(pl.multiple_of(y * tokens, tokens), tokens)
     summed = [[], []]
 
-    def combine(which):
-        for copy in back[which][:-1]:
+    def combine(group):
+        which = min(group, 1)
+        for copy in back[group][:-1]:
             copy.wait_recv()
-        back[which][-1].wait()
-        if which == 0:
+        back[group][-1].wait()
+        if group == 0:
             for copy in back[0][:-1]:
                 copy.wait_send()
         blocks = which * RINGS * tokens
@@ -530,20 +553,25 @@
             at = columns(n)
             rows = ret[which, :, :, at].reshape(rows_all, TILE)
             if which == 0:
-                total = lax.dot_general(whi[...], rows, CONTRACT_ROWS, preferred_element_type=F32)
-                total += lax.dot_general(wlo[...], rows, CONTRACT_ROWS, preferred_element_type=F32)
+                total = jnp.dot(whi[...], rows, preferred_element_type=F32)
+                total += jnp.dot(wlo[...], rows, preferred_element_type=F32)
             else:
-                total = lax.dot_general(pick[...], rows, CONTRACT_ROWS, preferred_element_type=F32)
+                total = jnp.dot(pick[...], rows, preferred_element_type=F32)
             acc[...] = total
             part[blocks : blocks + RINGS * tokens, at] = total.astype(BF16)
             own[which, :, at] = acc[own_rows, :]
             return 0
 
-        lax.fori_loop(0, width // TILE, step, 0)
+        first, size = spans[group].start, spans[group].size
+        lax.fori_loop(first // TILE, (first + size) // TILE, step, 0)
         for d in range(3):
             there = pl.ds(pl.multiple_of(blocks + lax.rem(y + d + 1, RINGS) * tokens, tokens), tokens)
             copy = remote(
-                part.at[there], gath.at[which, d], b_send.at[which, d], b_recv.at[which, d], ring[d]
+                part.at[there, spans[group]],
+                gath.at[which, d, :, spans[group]],
+                b_send.at[group, d],
+                b_recv.at[group, d],
+                ring[d],
             )
             copy.start()
             summed[which].append(copy)
@@ -588,6 +616,7 @@
             copy.start()
 
     combine(1)
+    combine(2)
 
     @pl.when(even)
     def _():
@@ -606,13 +635,14 @@
 
     for which, out in enumerate((mixed, input_grad)):
         total = own[which]
+        for copy in summed[which]:
+            copy.wait_recv()
         for d in range(3):
-            summed[which][d].wait_recv()
             total += gath[which, d].astype(F32)
         out[...] = total.astype(BF16)
     for copy in kept:
         copy.wait()
-    for copy in back[1][:-1] + x_copies + summed[0] + summed[1]:
+    for copy in back[1][:-1] + back[2][:-1] + x_copies + summed[0] + summed[1]:
         copy.wait_send()
 
 
@@ -648,9 +678,9 @@
             pltpu.VMEM((rows, 2 * ff), BF16),
             row_buffer,
             pltpu.VMEM((2, PLANE, ROWS, width), BF16),
-            pltpu.VMEM((rows, 512), BF16),
-            pltpu.VMEM((rows, 512), BF16),
-            pltpu.VMEM((rows, 512), BF16),
+            pltpu.VMEM((512, rows), BF16),
+            pltpu.VMEM((512, rows), BF16),
+            pltpu.VMEM((512, rows), BF16),
             pltpu.VMEM((512, TILE), F32),
             pltpu.VMEM((2 * 512, width), BF16),
             pltpu.VMEM((2, 128, width), F32),
@@ -659,7 +689,7 @@
             *slabs,
             *slabs,
             dma((7,)), dma((chunks,)), dma((chunks,)), dma((chunks,)), dma((chunks,)), dma((chunks,)),
-            dma((2,)), dma((2, 15)), dma((2, 15)), dma((2, 3)), dma((2, 3)),
+            dma((3,)), dma((3, 15)), dma((3, 15)), dma((3, 3)), dma((3, 3)),
         ],
         compiler_params=pltpu.CompilerParams(
             collective_id=1, has_side_effects=True, vmem_limit_bytes=63 * 2**20

time: 256 us -> 252 us (0.984)
  Pallas kernels: 245 us -> 240 us
    pallas_call x1, Pallas kernels: 122 us -> 119 us  [finish(): pl.pallas_call(finish_kernel, name='finish', out_shape=(row_shape, row_sh...]
where the time goes in v5:
time: 252 us; the launch traced here: 251 us
  Pallas kernels  240 us (95%)
  other arithmetic  7.41 us (3%)
    pallas_call x1, Pallas kernels, dispatch(): pl.pallas_call(dispatch_kernel, name='dispatch', out_shape=(row_shape, ro...  121 us
    pallas_call x1, Pallas kernels, finish(): pl.pallas_call(finish_kernel, name='finish', out_shape=(row_shape, row_sh...  119 us
    broadcast_in_dim x2, other arithmetic, body(): g.astype(F32)[None]  6.73 us

profile of v5, /device:TPU:1, one launch (start us, length us, event | category | flops | bytes accessed | tf_op | source)
XLA Modules:
  0.0 250.6 jit_solution(10166070693483764252)
XLA Ops:
  0.6 0.7 pad_add_fusion
  1.3 0.7 copy.16.table
  2.0 121.2 %dispatch.1 = (bf16[16,48,2048]{2,1,0:T(8,128)(2,1)}, bf16[16,48,2048]{2,1,0:T(8,128)(2,1)}, f32[4,8,128]{2,1,0:T(8,128)}, f32[768,1536]{1,0:T(8,128)}, bf16[768...) custom-call(s32[4,128]{1,0:T(4,128)} %bitcast.19, ...), custom_call_target="tpu_custom_call" | custom-call | tf_op jit(solution)/shard_map/dispatch/pallas_call | solution.py:338
  123.3 119.0 %finish.1 = (bf16[128,2048]{1,0:T(8,128)(2,1)}, bf16[128,2048]{1,0:T(8,128)(2,1)}, bf16[384,2048]{1,0:T(8,128)(2,1)}, bf16[1024,1536]{1,0:T(8,128)(2,1)}) custom-call(bf16[16,48,2048]{2,1,0:T(8,128)(2,1)} %get-tuple-element.17.x_in, bf16[16,48,2048]{2,1,0:T(8,128)(2,1)} %get-tuple-element.18.og_in, f32[768,1536]{1,0:T(8,128)} %get-tuple-element.19.pre_in, ...), custom_call_target="tpu_custom_call" | custom-call | tf_op jit(solution)/shard_map/finish/pallas_call | solution.py:665
  242.3 0.0 copy-start
  242.3 3.6 %bitcast_convert_fusion = f32[1,384,2048]{2,1,0:T(8,128)} fusion(bf16[384,2048]{1,0:T(8,128)(2,1)} %get-tuple-element.28), kind=kLoop, calls=%fused_computation | loop fusion | flops 786432 | bytes 4718592 | tf_op jit(solution)/shard_map/broadcast_in_dim | solution.py:709
  245.9 0.0 copy-done
  245.9 0.0 copy-start.2
  245.9 0.0 copy-start.1
  245.9 3.1 %bitcast_convert_fusion.1 = (f32[1,1024,768]{2,1,0:T(8,128)}, f32[1,1024,768]{2,1,0:T(8,128)}) fusion(bf16[1024,1536]{1,0:T(8,128)(2,1)S(1)} %copy-done), kind=kLoop, calls=%fused_computation.1 | loop fusion | flops 1572864 | bytes 9437184 | tf_op jit(solution)/shard_map/broadcast_in_dim | solution.py:709
  249.0 0.0 copy-done.2
  249.0 0.8 copy.20
  249.8 0.0 copy-done.1
  249.8 0.8 copy.21
Async XLA Ops:
  242.3 3.6 %copy-start = (bf16[1024,1536]{1,0:T(8,128)(2,1)S(1)}, bf16[1024,1536]{1,0:T(8,128)(2,1)}, u32[]{:S(2)}) copy-start(bf16[1024,1536]{1,0:T(8,128)(2,1)} %get-tuple-element.27) | copy-start | bytes 9437188
  245.9 3.1 %copy-start.2 = (bf16[128,2048]{1,0:T(8,128)(2,1)S(1)}, bf16[128,2048]{1,0:T(8,128)(2,1)}, u32[]{:S(2)}) copy-start(bf16[128,2048]{1,0:T(8,128)(2,1)} %get-tuple-element.36) | copy-start | bytes 1572868
  245.9 3.9 %copy-start.1 = (bf16[128,2048]{1,0:T(8,128)(2,1)S(1)}, bf16[128,2048]{1,0:T(8,128)(2,1)}, u32[]{:S(2)}) copy-start(bf16[128,2048]{1,0:T(8,128)(2,1)} %get-tuple-element.37) | copy-start | bytes 1572868

commit v6 on v5

--- a/solution.py
+++ b/solution.py
@@ -427,7 +427,7 @@
         left = x[:, :, at].reshape(rows_all, WIDE).T
         return lambda cols: jnp.dot(left, gu[:, cols], preferred_element_type=F32)
 
-    spans = [pl.ds(0, width), pl.ds(0, width // 2), pl.ds(width // 2, width // 2)]
+    spans = [pl.ds(0, width)] + [pl.ds(i * (width // 4), width // 4) for i in range(4)]
 
     def returned(group, j):
         if group == 0:
@@ -437,8 +437,8 @@
     def landing(group):
         return ret.at[0, l] if group == 0 else ret.at[1, l, :, spans[group]]
 
-    back = [[], [], []]
-    for group in range(3):
+    back = [[] for _ in spans]
+    for group in range(len(spans)):
         for r, (device, j) in enumerate(peers):
             back[group].append(
                 remote(
@@ -525,7 +525,7 @@
         return 0
 
     lax.fori_loop(0, width // TILE, pull, 0)
-    for copy in back[1] + back[2]:
+    for copy in [b for group in back[1:] for b in group]:
         copy.start()
     for b in range(RINGS):
         hit, weight = selection(meta, y * PLANE * ROWS, b)
@@ -615,8 +615,8 @@
         for copy in x_copies:
             copy.start()
 
-    combine(1)
-    combine(2)
+    for group in range(1, len(spans)):
+        combine(group)
 
     @pl.when(even)
     def _():
@@ -642,7 +642,7 @@
         out[...] = total.astype(BF16)
     for copy in kept:
         copy.wait()
-    for copy in back[1][:-1] + back[2][:-1] + x_copies + summed[0] + summed[1]:
+    for copy in [b for group in back[1:] for b in group[:-1]] + x_copies + summed[0] + summed[1]:
         copy.wait_send()
 
 
@@ -689,7 +689,7 @@
             *slabs,
             *slabs,
             dma((7,)), dma((chunks,)), dma((chunks,)), dma((chunks,)), dma((chunks,)), dma((chunks,)),
-            dma((3,)), dma((3, 15)), dma((3, 15)), dma((3, 3)), dma((3, 3)),
+            dma((5,)), dma((5, 15)), dma((5, 15)), dma((5, 3)), dma((5, 3)),
         ],
         compiler_params=pltpu.CompilerParams(
             collective_id=1, has_side_effects=True, vmem_limit_bytes=63 * 2**20

time: 252 us -> 253 us (level)
  no operation moved by 1% of the time
where the time goes in v6:
time: 253 us; the launch traced here: 251 us
  Pallas kernels  241 us (95%)
  other arithmetic  7.41 us (3%)
    pallas_call x1, Pallas kernels, dispatch(): pl.pallas_call(dispatch_kernel, name='dispatch', out_shape=(row_shape, ro...  121 us
    pallas_call x1, Pallas kernels, finish(): pl.pallas_call(finish_kernel, name='finish', out_shape=(row_shape, row_sh...  120 us
    broadcast_in_dim x2, other arithmetic, body(): g.astype(F32)[None]  6.73 us

profile of v6, /device:TPU:1, one launch (start us, length us, event | category | flops | bytes accessed | tf_op | source)
XLA Modules:
  0.0 251.4 jit_solution(5655600267079306394)
XLA Ops:
  0.6 0.7 pad_add_fusion
  1.3 0.7 copy.16.table
  2.0 121.2 %dispatch.1 = (bf16[16,48,2048]{2,1,0:T(8,128)(2,1)}, bf16[16,48,2048]{2,1,0:T(8,128)(2,1)}, f32[4,8,128]{2,1,0:T(8,128)}, f32[768,1536]{1,0:T(8,128)}, bf16[768...) custom-call(s32[4,128]{1,0:T(4,128)} %bitcast.19, ...), custom_call_target="tpu_custom_call" | custom-call | tf_op jit(solution)/shard_map/dispatch/pallas_call | solution.py:338
  123.3 119.8 %finish.1 = (bf16[128,2048]{1,0:T(8,128)(2,1)}, bf16[128,2048]{1,0:T(8,128)(2,1)}, bf16[384,2048]{1,0:T(8,128)(2,1)}, bf16[1024,1536]{1,0:T(8,128)(2,1)}) custom-call(bf16[16,48,2048]{2,1,0:T(8,128)(2,1)} %get-tuple-element.17.x_in, bf16[16,48,2048]{2,1,0:T(8,128)(2,1)} %get-tuple-element.18.og_in, f32[768,1536]{1,0:T(8,128)} %get-tuple-element.19.pre_in, ...), custom_call_target="tpu_custom_call" | custom-call | tf_op jit(solution)/shard_map/finish/pallas_call | solution.py:665
  243.0 0.0 copy-start
  243.0 3.6 %bitcast_convert_fusion = f32[1,384,2048]{2,1,0:T(8,128)} fusion(bf16[384,2048]{1,0:T(8,128)(2,1)} %get-tuple-element.28), kind=kLoop, calls=%fused_computation | loop fusion | flops 786432 | bytes 4718592 | tf_op jit(solution)/shard_map/broadcast_in_dim | solution.py:709
  246.6 0.0 copy-done
  246.6 0.0 copy-start.2
  246.6 0.0 copy-start.1
  246.6 3.1 %bitcast_convert_fusion.1 = (f32[1,1024,768]{2,1,0:T(8,128)}, f32[1,1024,768]{2,1,0:T(8,128)}) fusion(bf16[1024,1536]{1,0:T(8,128)(2,1)S(1)} %copy-done), kind=kLoop, calls=%fused_computation.1 | loop fusion | flops 1572864 | bytes 9437184 | tf_op jit(solution)/shard_map/broadcast_in_dim | solution.py:709
  249.8 0.0 copy-done.2
  249.8 0.8 copy.20
  250.6 0.0 copy-done.1
  250.6 0.8 copy.21
Async XLA Ops:
  243.0 3.6 %copy-start = (bf16[1024,1536]{1,0:T(8,128)(2,1)S(1)}, bf16[1024,1536]{1,0:T(8,128)(2,1)}, u32[]{:S(2)}) copy-start(bf16[1024,1536]{1,0:T(8,128)(2,1)} %get-tuple-element.27) | copy-start | bytes 9437188
  246.6 3.1 %copy-start.2 = (bf16[128,2048]{1,0:T(8,128)(2,1)S(1)}, bf16[128,2048]{1,0:T(8,128)(2,1)}, u32[]{:S(2)}) copy-start(bf16[128,2048]{1,0:T(8,128)(2,1)} %get-tuple-element.36) | copy-start | bytes 1572868
  246.6 3.9 %copy-start.1 = (bf16[128,2048]{1,0:T(8,128)(2,1)S(1)}, bf16[128,2048]{1,0:T(8,128)(2,1)}, u32[]{:S(2)}) copy-start(bf16[128,2048]{1,0:T(8,128)(2,1)} %get-tuple-element.37) | copy-start | bytes 1572868
